TPU v7x, 32 devices: a whole 2x2x4 slice. The times are simulated.
32 devices in a mesh: dp: 8 (over z, x), tensor: 4 (over y, core).
Axes of the slice: x: 2, y: 2, z: 4, core: 2. Of those that a mesh axis runs over, the one named last changes fastest.
Arguments:
- text_in: bfloat16 [32, 512, 768], P(('dp', 'tensor')), may hold values from -6 to 6
- layout_in: bfloat16 [32, 512, 192], P(('dp', 'tensor')), may hold values from -6 to 6
- lengths: int32 [32], P('dp'), may hold values from 128 to 512, as said below
- text_mask: int32 [32, 512], P(('dp', 'tensor')), may hold values 0 or 1
- box_mask: int32 [32, 512], P(('dp', 'tensor')), may hold values from 0 to 1, as said below
- text_cot: bfloat16 [32, 512, 768], P(('dp', 'tensor')), may hold values from -6 to 6
- layout_cot: bfloat16 [32, 512, 192], P(('dp', 'tensor')), may hold values from -6 to 6
- master: float32 [4, 8, 235008], P('tensor', 'dp')
- first_moment: float32 [4, 8, 235008], P('tensor', 'dp')
- second_moment: float32 [4, 8, 235008], P('tensor', 'dp'), as said below
- ema_weights: float32 [4, 8, 235008], P('tensor', 'dp')
- vectors: float32 [12480], replicated
- vector_first: float32 [12480], replicated
- vector_second: float32 [12480], replicated
- vector_ema: float32 [12480], replicated
Outputs:
- text_out: bfloat16 [32, 512, 768], P(('dp', 'tensor'))
- layout_out: bfloat16 [32, 512, 192], P(('dp', 'tensor'))
- text_in_grad: float32 [32, 512, 768], P(('dp', 'tensor'))
- layout_in_grad: float32 [32, 512, 192], P(('dp', 'tensor'))
- grad_norm: float32 [], replicated
- new_master: float32 [4, 8, 235008], P('tensor', 'dp')
- new_first: float32 [4, 8, 235008], P('tensor', 'dp')
- new_second: float32 [4, 8, 235008], P('tensor', 'dp')
- master_bf16: bfloat16 [4, 8, 235008], P('tensor', 'dp')
- new_ema: float32 [4, 8, 235008], P('tensor', 'dp')
- new_vectors: float32 [12480], replicated
- new_vector_first: float32 [12480], replicated
- new_vector_second: float32 [12480], replicated
- vectors_bf16: bfloat16 [12480], replicated
- new_vector_ema: float32 [12480], replicated
Inputs may be any that keep to these rules, and one draw needn't show every extreme that they name: `lengths`: each page has between 128 and 512 valid positions; some page is full and some has 128. `box_mask`: masked boxes come singly and as whole aligned regions of 8 positions. `second_moment`: second moments are positive.
All inputs are finite; a program needn't handle non-finite values. No bound on the sum of `text_mask` on one device may be relied on, other than what follows from the above.
Results may differ from a plain program's by a relative error of at most 0.012.
The roundings to bfloat16 on the way count: a program that leaves them out, or rounds other values in their place, can miss the bound.
Values may be sent and summed in bfloat16 or wider, within the bound.
No kernel may reach another device: no remote copies, remote signals or barrier semaphores. Data moves between devices by JAX's collectives and lax.ppermute only.
A program may use at most 192 MiB of HBM per device.

v0:
```python
from functools import partial
import math

import jax
import jax.numpy as jnp
from jax import lax
from jax.sharding import PartitionSpec as P

D = 768
HT = 64
FF = 3072
L = 192
HL = 16
LF = 768
STEP = 5


norm_eps = 1e-05
clip_bound = 1.0
first_decay = 0.5
second_decay = 0.6
adam_floor = 1e-08
weight_decay = 0.01
vector_rate = 0.5
average_keep = 0.5
masked_score = -1e30


def piece_table(parts):
    text_spread = 1.0 / math.sqrt(D)
    layout_spread = 1.0 / math.sqrt(L)
    return [
        (D, D // parts, text_spread),
        (D, D // parts, text_spread),
        (D, D // parts, text_spread),
        (D // parts, D, 8.0 * text_spread),
        (D, FF // parts, text_spread),
        (FF // parts, D, 1.0 / math.sqrt(FF)),
        (L, L // parts, layout_spread),
        (L, L // parts, layout_spread),
        (L, L // parts, layout_spread),
        (L // parts, L, 8.0 * layout_spread),
        (L, LF // parts, layout_spread),
        (LF // parts, L, 1.0 / math.sqrt(LF)),
    ]


def split_pieces(flat, parts):
    pieces = []
    start = 0
    for height, width, spread in piece_table(parts):
        pieces.append(flat[start : start + height * width].reshape(height, width))
        start = start + height * width
    return pieces


def rate_table(parts):
    return jnp.concatenate(
        [
            jnp.full((height * width,), spread, jnp.float32)
            for height, width, spread in piece_table(parts)
        ]
    )


def split_vector(flat):
    pieces = []
    start = 0
    for width in [D] * 8 + [FF] + [L] * 8 + [LF] + [D, L]:
        pieces.append(flat[start : start + width])
        start = start + width
    return pieces


def project(acts, weight):
    return jnp.einsum("psd,de->pse", acts, weight, preferred_element_type=jnp.float32)


def project_back(incoming, weight):
    return jnp.einsum("pse,de->psd", incoming, weight, preferred_element_type=jnp.float32)


def weight_grad(acts, incoming):
    return jnp.einsum("psd,pse->de", acts, incoming, preferred_element_type=jnp.float32)


def norm_forward(value, gain, shift):
    mean = jnp.mean(value, -1, keepdims=True)
    centred = value - mean
    scale = lax.rsqrt(jnp.mean(centred * centred, -1, keepdims=True) + norm_eps)
    normed = centred * scale
    return (normed * gain + shift, normed, scale)


def norm_backward(incoming, normed, scale, gain):
    scaled = incoming * gain
    result = scale * (
        scaled
        - jnp.mean(scaled, -1, keepdims=True)
        - normed * jnp.mean(scaled * normed, -1, keepdims=True)
    )
    return (result, jnp.sum(incoming * normed, (0, 1)), jnp.sum(incoming, (0, 1)))


def gelu_back(value, incoming):
    unused, pull = jax.vjp(partial(jax.nn.gelu, approximate=False), value)
    return pull(incoming)[0]


def joint_scores(text_query, text_key, layout_query, layout_key, length):
    positions = text_query.shape[0]
    text_raw = jnp.einsum(
        "qhd,khd->hqk",
        text_query.reshape(positions, -1, HT),
        text_key.reshape(positions, -1, HT),
        preferred_element_type=jnp.float32,
    ) * (1.0 / math.sqrt(HT))
    layout_raw = jnp.einsum(
        "qhd,khd->hqk",
        layout_query.reshape(positions, -1, HL),
        layout_key.reshape(positions, -1, HL),
        preferred_element_type=jnp.float32,
    ) * (1.0 / math.sqrt(HL))
    valid = jnp.arange(positions) < length
    return jnp.where(valid, text_raw + layout_raw, masked_score)


def attend_page(items):
    text_query, text_key, text_value, layout_query, layout_key, layout_value, length = items
    positions = text_query.shape[0]
    scores = joint_scores(text_query, text_key, layout_query, layout_key, length)
    top = jnp.max(scores, -1, keepdims=True)
    raised = jnp.exp(scores - top)
    total = jnp.sum(raised, -1, keepdims=True)
    probs = (raised / total).astype(jnp.bfloat16)
    text_context = jnp.einsum(
        "hqk,khd->qhd",
        probs,
        text_value.reshape(positions, -1, HT),
        preferred_element_type=jnp.float32,
    )
    layout_context = jnp.einsum(
        "hqk,khd->qhd",
        probs,
        layout_value.reshape(positions, -1, HL),
        preferred_element_type=jnp.float32,
    )
    return (
        text_context.reshape(positions, -1).astype(jnp.bfloat16),
        layout_context.reshape(positions, -1).astype(jnp.bfloat16),
        (top + jnp.log(total))[..., 0],
    )


def attend_back(items):
    (
        text_query,
        text_key,
        text_value,
        layout_query,
        layout_key,
        layout_value,
        length,
        log_total,
        text_incoming,
        layout_incoming,
    ) = items
    positions = text_query.shape[0]
    scores = joint_scores(text_query, text_key, layout_query, layout_key, length)
    probs = jnp.exp(scores - log_total[..., None])
    rounded = probs.astype(jnp.bfloat16)
    text_heads = text_incoming.reshape(positions, -1, HT)
    layout_heads = layout_incoming.reshape(positions, -1, HL)
    text_prob_grad = jnp.einsum(
        "qhd,khd->hqk",
        text_heads,
        text_value.reshape(positions, -1, HT),
        preferred_element_type=jnp.float32,
    )
    layout_prob_grad = jnp.einsum(
        "qhd,khd->hqk",
        layout_heads,
        layout_value.reshape(positions, -1, HL),
        preferred_element_type=jnp.float32,
    )
    text_score_grad = probs * (text_prob_grad - jnp.sum(probs * text_prob_grad, -1, keepdims=True))
    layout_score_grad = probs * (
        layout_prob_grad - jnp.sum(probs * layout_prob_grad, -1, keepdims=True)
    )
    joint_grad = (text_score_grad + layout_score_grad).astype(jnp.bfloat16)
    layout_only = layout_score_grad.astype(jnp.bfloat16)
    text_scale = 1.0 / math.sqrt(HT)
    layout_scale = 1.0 / math.sqrt(HL)
    text_query_grad = (
        jnp.einsum(
            "hqk,khd->qhd",
            joint_grad,
            text_key.reshape(positions, -1, HT),
            preferred_element_type=jnp.float32,
        )
        * text_scale
    )
    text_key_grad = (
        jnp.einsum(
            "hqk,qhd->khd",
            joint_grad,
            text_query.reshape(positions, -1, HT),
            preferred_element_type=jnp.float32,
        )
        * text_scale
    )
    text_value_grad = jnp.einsum(
        "hqk,qhd->khd", rounded, text_heads, preferred_element_type=jnp.float32
    )
    layout_query_grad = (
        jnp.einsum(
            "hqk,khd->qhd",
            layout_only,
            layout_key.reshape(positions, -1, HL),
            preferred_element_type=jnp.float32,
        )
        * layout_scale
    )
    layout_key_grad = (
        jnp.einsum(
            "hqk,qhd->khd",
            layout_only,
            layout_query.reshape(positions, -1, HL),
            preferred_element_type=jnp.float32,
        )
        * layout_scale
    )
    layout_value_grad = jnp.einsum(
        "hqk,qhd->khd", rounded, layout_heads, preferred_element_type=jnp.float32
    )
    results = (
        text_query_grad,
        text_key_grad,
        text_value_grad,
        layout_query_grad,
        layout_key_grad,
        layout_value_grad,
    )
    return tuple((item.reshape(positions, -1).astype(jnp.bfloat16) for item in results))


def adam_update(weight, gradient, first, second, average, rate, factor):
    clipped = gradient * factor
    new_first = first_decay * first + (1.0 - first_decay) * clipped
    new_second = second_decay * second + (1.0 - second_decay) * clipped * clipped
    first_hat = new_first / (1.0 - first_decay**STEP)
    second_hat = new_second / (1.0 - second_decay**STEP)
    updated = weight - rate * (
        first_hat / (jnp.sqrt(second_hat) + adam_floor) + weight_decay * weight
    )
    return (
        updated,
        new_first,
        new_second,
        updated.astype(jnp.bfloat16),
        average_keep * average + (1.0 - average_keep) * updated,
    )


def shards(
    text_in,
    layout_in,
    lengths,
    text_mask,
    box_mask,
    text_cot,
    layout_cot,
    master,
    first_moment,
    second_moment,
    ema_weights,
    vectors,
    vector_first,
    vector_second,
    vector_ema,
):
    parts = lax.axis_size("tensor")
    tensor_index = lax.axis_index("tensor")
    dp_index = lax.axis_index("dp")
    own_pages = text_in.shape[0]
    wire = master.astype(jnp.bfloat16)
    gathered = lax.all_gather(wire, "dp", axis=1, tiled=True)
    weights = split_pieces(gathered.reshape(-1), parts)
    biases = split_vector(vectors)

    def local_part(vector, width):
        return lax.dynamic_slice_in_dim(vector, tensor_index * width, width)

    def placed(piece, width):
        return lax.dynamic_update_slice_in_dim(
            jnp.zeros((width,), jnp.float32), piece, tensor_index * piece.shape[0], 0
        )

    def summed(value):
        return jnp.sum(value, (0, 1), dtype=jnp.float32)

    def head_total(term_fn):
        joined = lax.psum_scatter(
            term_fn(jnp.int32(0), own_pages * lax.axis_size("tensor")),
            "tensor",
            scatter_dimension=0,
            tiled=True,
        )
        return (joined[..., :D], joined[..., D:])

    text_flag = (text_mask > 0)[..., None]
    box_flag = (box_mask > 0)[..., None]
    text_act = jnp.where(text_flag, biases[18], text_in.astype(jnp.float32))
    layout_act = jnp.where(box_flag, biases[19], layout_in.astype(jnp.float32))
    text_all, layout_all = (
        lax.all_gather(text_act.astype(jnp.bfloat16), "tensor", axis=0, tiled=True),
        lax.all_gather(layout_act.astype(jnp.bfloat16), "tensor", axis=0, tiled=True),
    )
    text_query = (project(text_all, weights[0]) + local_part(biases[0], D // parts)).astype(
        jnp.bfloat16
    )
    text_key = project(text_all, weights[1]).astype(jnp.bfloat16)
    text_value = (project(text_all, weights[2]) + local_part(biases[1], D // parts)).astype(
        jnp.bfloat16
    )
    layout_query = (project(layout_all, weights[6]) + local_part(biases[9], L // parts)).astype(
        jnp.bfloat16
    )
    layout_key = project(layout_all, weights[7]).astype(jnp.bfloat16)
    layout_value = (project(layout_all, weights[8]) + local_part(biases[10], L // parts)).astype(
        jnp.bfloat16
    )
    text_context, layout_context, log_total = lax.map(
        attend_page,
        (text_query, text_key, text_value, layout_query, layout_key, layout_value, lengths),
    )

    def attn_term(start, count):
        return jnp.concatenate(
            (project(text_context, weights[3]), project(layout_context, weights[9])), -1
        )

    text_attn, layout_attn = head_total(attn_term)
    text_mid, text_normed_one, text_scale_one = norm_forward(
        text_attn + biases[2] + text_act, biases[3], biases[4]
    )
    layout_mid, layout_normed_one, layout_scale_one = norm_forward(
        layout_attn + biases[11] + layout_act, biases[12], biases[13]
    )
    text_mid_all, layout_mid_all = (
        lax.all_gather(text_mid.astype(jnp.bfloat16), "tensor", axis=0, tiled=True),
        lax.all_gather(layout_mid.astype(jnp.bfloat16), "tensor", axis=0, tiled=True),
    )
    text_up = project(text_mid_all, weights[4]) + local_part(biases[8], FF // parts)
    layout_up = project(layout_mid_all, weights[10]) + local_part(biases[17], LF // parts)
    text_hidden = jax.nn.gelu(text_up, approximate=False).astype(jnp.bfloat16)
    layout_hidden = jax.nn.gelu(layout_up, approximate=False).astype(jnp.bfloat16)

    def down_term(start, count):
        return jnp.concatenate(
            (project(text_hidden, weights[5]), project(layout_hidden, weights[11])), -1
        )

    text_down, layout_down = head_total(down_term)
    text_final, text_normed_two, text_scale_two = norm_forward(
        text_down + biases[5] + text_mid, biases[6], biases[7]
    )
    layout_final, layout_normed_two, layout_scale_two = norm_forward(
        layout_down + biases[14] + layout_mid, biases[15], biases[16]
    )
    text_pre_two, text_gain_two, text_shift_two = norm_backward(
        text_cot.astype(jnp.float32), text_normed_two, text_scale_two, biases[6]
    )
    layout_pre_two, layout_gain_two, layout_shift_two = norm_backward(
        layout_cot.astype(jnp.float32), layout_normed_two, layout_scale_two, biases[15]
    )
    text_down_in, layout_down_in = (
        lax.all_gather(text_pre_two.astype(jnp.bfloat16), "tensor", axis=0, tiled=True),
        lax.all_gather(layout_pre_two.astype(jnp.bfloat16), "tensor", axis=0, tiled=True),
    )
    text_up_grad = gelu_back(text_up, project_back(text_down_in, weights[5])).astype(jnp.bfloat16)
    layout_up_grad = gelu_back(layout_up, project_back(layout_down_in, weights[11])).astype(
        jnp.bfloat16
    )

    def up_term(start, count):
        return jnp.concatenate(
            (project_back(text_up_grad, weights[4]), project_back(layout_up_grad, weights[10])), -1
        )

    text_mid_back, layout_mid_back = head_total(up_term)
    text_pre_one, text_gain_one, text_shift_one = norm_backward(
        text_pre_two + text_mid_back, text_normed_one, text_scale_one, biases[3]
    )
    layout_pre_one, layout_gain_one, layout_shift_one = norm_backward(
        layout_pre_two + layout_mid_back, layout_normed_one, layout_scale_one, biases[12]
    )
    text_attn_in, layout_attn_in = (
        lax.all_gather(text_pre_one.astype(jnp.bfloat16), "tensor", axis=0, tiled=True),
        lax.all_gather(layout_pre_one.astype(jnp.bfloat16), "tensor", axis=0, tiled=True),
    )
    text_context_grad = project_back(text_attn_in, weights[3]).astype(jnp.bfloat16)
    layout_context_grad = project_back(layout_attn_in, weights[9]).astype(jnp.bfloat16)
    attention_grads = lax.map(
        attend_back,
        (
            text_query,
            text_key,
            text_value,
            layout_query,
            layout_key,
            layout_value,
            lengths,
            log_total,
            text_context_grad,
            layout_context_grad,
        ),
    )
    (
        text_query_grad,
        text_key_grad,
        text_value_grad,
        layout_query_grad,
        layout_key_grad,
        layout_value_grad,
    ) = attention_grads

    def input_term(start, count):
        text_part = (
            project_back(text_query_grad, weights[0])
            + project_back(text_key_grad, weights[1])
            + project_back(text_value_grad, weights[2])
        )
        layout_part = (
            project_back(layout_query_grad, weights[6])
            + project_back(layout_key_grad, weights[7])
            + project_back(layout_value_grad, weights[8])
        )
        return jnp.concatenate((text_part, layout_part), -1)

    text_input_back, layout_input_back = head_total(input_term)
    text_full = text_pre_one + text_input_back
    layout_full = layout_pre_one + layout_input_back
    text_in_grad = jnp.where(text_flag, 0.0, text_full)
    layout_in_grad = jnp.where(box_flag, 0.0, layout_full)
    text_embed_grad = summed(jnp.where(text_flag, text_full, 0.0))
    layout_embed_grad = summed(jnp.where(box_flag, layout_full, 0.0))
    matrix_grads = [
        weight_grad(text_all, text_query_grad),
        weight_grad(text_all, text_key_grad),
        weight_grad(text_all, text_value_grad),
        weight_grad(text_context, text_attn_in),
        weight_grad(text_mid_all, text_up_grad),
        weight_grad(text_hidden, text_down_in),
        weight_grad(layout_all, layout_query_grad),
        weight_grad(layout_all, layout_key_grad),
        weight_grad(layout_all, layout_value_grad),
        weight_grad(layout_context, layout_attn_in),
        weight_grad(layout_mid_all, layout_up_grad),
        weight_grad(layout_hidden, layout_down_in),
    ]
    flat_grad = jnp.concatenate([item.reshape(-1) for item in matrix_grads]).reshape(gathered.shape)
    span_grad = lax.psum_scatter(flat_grad, "dp", scatter_dimension=1, tiled=True)
    vector_part = jnp.concatenate(
        [
            placed(summed(text_query_grad), D),
            placed(summed(text_value_grad), D),
            summed(text_pre_one),
            text_gain_one,
            text_shift_one,
            summed(text_pre_two),
            text_gain_two,
            text_shift_two,
            placed(summed(text_up_grad), FF),
            placed(summed(layout_query_grad), L),
            placed(summed(layout_value_grad), L),
            summed(layout_pre_one),
            layout_gain_one,
            layout_shift_one,
            summed(layout_pre_two),
            layout_gain_two,
            layout_shift_two,
            placed(summed(layout_up_grad), LF),
            text_embed_grad,
            layout_embed_grad,
        ]
    )
    local_square = jnp.sum(span_grad * span_grad)
    vector_grad = lax.psum(vector_part, ("dp", "tensor"))
    matrix_square = lax.psum(local_square, ("dp", "tensor"))
    grad_norm = jnp.sqrt(matrix_square + jnp.sum(vector_grad * vector_grad))
    factor = clip_bound / jnp.maximum(grad_norm, clip_bound)
    span = master.shape[2]
    rates = lax.dynamic_slice_in_dim(rate_table(parts), dp_index * span, span).reshape(master.shape)
    matrix_new = adam_update(
        master, span_grad, first_moment, second_moment, ema_weights, rates, factor
    )
    vector_new = adam_update(
        vectors, vector_grad, vector_first, vector_second, vector_ema, vector_rate, factor
    )
    return (
        (
            text_final.astype(jnp.bfloat16),
            layout_final.astype(jnp.bfloat16),
            text_in_grad,
            layout_in_grad,
            grad_norm,
        )
        + matrix_new
        + vector_new
    )


def solution(mesh):
    in_specs = (
        P(("dp", "tensor"), None, None),
        P(("dp", "tensor"), None, None),
        P("dp"),
        P(("dp", "tensor"), None),
        P(("dp", "tensor"), None),
        P(("dp", "tensor"), None, None),
        P(("dp", "tensor"), None, None),
        P("tensor", "dp", None),
        P("tensor", "dp", None),
        P("tensor", "dp", None),
        P("tensor", "dp", None),
        P(),
        P(),
        P(),
        P(),
    )
    out_specs = (
        P(("dp", "tensor"), None, None),
        P(("dp", "tensor"), None, None),
        P(("dp", "tensor"), None, None),
        P(("dp", "tensor"), None, None),
        P(),
        P("tensor", "dp", None),
        P("tensor", "dp", None),
        P("tensor", "dp", None),
        P("tensor", "dp", None),
        P("tensor", "dp", None),
        P(),
        P(),
        P(),
        P(),
        P(),
    )
    return jax.shard_map(shards, mesh=mesh, in_specs=in_specs, out_specs=out_specs, check_vma=False)
```

profile of v0, /device:TPU:0, one launch (start us, length us, event | category | flops | bytes accessed | tf_op | source)
XLA Modules:
  0.0 1241.0 jit_solution(13413750543774267479)
XLA Ops:
  13.5 10.1 all_gather.29
  23.5 104.2 %all-gather.8.cloned.1.call-done = bf16[1,8,235008]{2,0,1:T(2,128)(2,1)} async-done(((bf16[1,1,235008]{2,0,1:T(2,128)(2,1)}), bf16[1,8,235008]{2,0,1:T(2,128)(2,1)}) %all-gather.8.cloned.1.call-update) | async-done | bytes 3760144 | tf_op jit(solution)/shard_map/all_gather | solution.py:287
  127.7 69.3 %reduce.17 = bf16[8,235008]{1,0:T(8,128)(2,1)} reduce(bf16[1,8,235008]{2,0,1:T(2,128)(2,1)} %all-gather.8.cloned.1.call-done, bf16[]{:T(256)} %constant.265), dimensions={0}, to_apply=%all_gather.28.reduce_sub_computation | reduce | bytes 7520258 | tf_op jit(solution)/shard_map/all_gather | solution.py:287
  197.0 9.4 reshape.549
  206.5 8.4 slice.139
  214.9 14.5 %slice.146 = bf16[39168,48]{1,0:T(8,128)(2,1)} reshape(bf16[1880064]{0:T(1024)(128)(2,1)} %reshape.549) | data formatting | bytes 7520256 | tf_op jit(solution)/shard_map/slice | solution.py:52
  229.3 9.5 slice.152
  244.1 4.2 convolution_convert_fusion.5
  253.6 31.7 %while.34 = (s32[]{:T(128)}, bf16[4,512,192]{1,2,0:T(8,128)(2,1)S(1)}, bf16[4,512,48]{1,2,0:T(8,128)(2,1)S(1)}, f32[4,3,512]{2,1,0:T(4,128)}, bf16[4,512,192]{1,...) while((s32[]{:T(128)}, ...), condition=%wide.region_3.4_spmd, body=%wide.region_0.3_spmd.sunk | while | flops 259644416 | bytes 23449244 | solution.py:333
  288.8 4.0 pad_maximum_fusion
  292.9 67.3 %reduce-scatter.6.cloned.1.call-done = f32[1,512,960]{1,2,0:T(8,128)} async-done(((f32[4,512,960]{1,2,0:T(8,128)}), f32[1,512,960]{1,2,0:T(8,128)}) %reduce-scatter.6.cloned.1.call-update) | async-done | bytes 1966096 | tf_op jit(solution)/shard_map/reduce_scatter | solution.py:303
  366.0 8.2 all_gather.31
  377.1 4.6 multiply_convert_fusion.1
  384.1 8.3 all-gather.10.cloned.1.call-done
  392.4 6.5 fusion.55
  398.9 15.4 %multiply_convert_fusion = (bf16[4,512,768]{2,1,0:T(8,128)(2,1)S(1)}, f32[4,512,768]{2,1,0:T(8,128)}) fusion(f32[4,512,768]{2,1,0:T(8,128)S(1)} %get-tuple-element.406, f32[768]{0:T(1024)S(1)} %copy-done.82, u8[512,768]{1,0:T(8,128)(4,1)S(1)} %get-tuple-element.251, u8[512,768]{1,0:T(8,128)(4,1)S(1)} %get-tuple-element.250), kind=kLoop, calls=%fused_computation.72 | loop fusion | flops 111673344 | bytes 16518144 | tf_op jit(solution)/shard_map/convert_element_type | solution.py:356
  414.3 4.9 fusion.62
  419.3 4.1 pad_maximum_fusion.1
  425.7 66.9 %reduce-scatter.8.cloned.1.call-done = f32[1,512,960]{1,2,0:T(8,128)} async-done(((f32[4,512,960]{1,2,0:T(8,128)}), f32[1,512,960]{1,2,0:T(8,128)}) %reduce-scatter.8.cloned.1.call-update) | async-done | bytes 1966096 | tf_op jit(solution)/shard_map/reduce_scatter | solution.py:303
  503.3 9.8 all_gather.33
  519.0 10.1 all-gather.12.cloned.1.call-done
  529.1 11.0 convert_reduce_fusion
  541.9 4.0 fusion.60
  545.9 4.0 pad_maximum_fusion.2
  551.7 67.8 %reduce-scatter.10.cloned.1.call-done = f32[1,512,960]{1,2,0:T(8,128)} async-done(((f32[4,512,960]{1,2,0:T(8,128)}), f32[1,512,960]{1,2,0:T(8,128)}) %reduce-scatter.10.cloned.1.call-update) | async-done | bytes 1966096 | tf_op jit(solution)/shard_map/reduce_scatter | solution.py:303
  619.4 4.8 fusion.45
  631.4 7.3 convolution_bitcast_fusion.1
  638.6 3.8 reshape.504
  642.5 6.1 convolution_bitcast_fusion
  648.6 3.3 reshape.505
  655.6 8.3 all_gather.35
  666.7 4.0 convolution_convert_fusion.4
  675.5 126.2 %while.35 = (s32[]{:T(128)}, bf16[4,512,192]{1,2,0:T(8,128)(2,1)}, bf16[4,512,192]{1,2,0:T(8,128)(2,1)}, bf16[4,512,192]{1,2,0:T(8,128)(2,1)}, bf16[4,512,48]{1,...) while((s32[]{:T(128)}, bf16[4,512,192]{1,2,0:T(8,128)(2,1)}, ...), condition=%wide.region_26.27_spmd, body=%wide.region_23.26_spmd.sunk | while | flops 650210304 | bytes 75150632 | solution.py:404
  693.2 6.2 fusion.256
  701.1 5.3 fusion.255
  724.7 6.2 fusion.256
  732.6 5.3 fusion.255
  756.2 6.2 fusion.256
  764.1 5.3 fusion.255
  787.7 6.2 fusion.256
  795.6 5.3 fusion.255
  839.5 8.4 reshape.512
  860.0 4.0 pad_maximum_fusion.3
  875.4 219.7 %all-reduce.4.cloned.1.call-done = f32[1,8,235008]{2,1,0:T(8,128)} async-done(((f32[1,8,235008]{2,1,0:T(8,128)}), f32[1,8,235008]{2,1,0:T(8,128)}) %all-reduce.4.cloned.1.call-update) | async-done | bytes 7520272
  1095.1 5.4 multiply_reduce_fusion.7
  1100.6 65.2 %reduce-scatter.12.cloned.1.call-done = f32[1,512,960]{1,2,0:T(8,128)} async-done(((f32[4,512,960]{1,2,0:T(8,128)}), f32[1,512,960]{1,2,0:T(8,128)}) %reduce-scatter.12.cloned.1.call-update) | async-done | bytes 1966096 | tf_op jit(solution)/shard_map/reduce_scatter | solution.py:303
  1172.1 40.2 %all-reduce.1 = (f32[]{:T(128)}, f32[12480]{0:T(1024)S(1)}) all-reduce(f32[]{:T(128)} %multiply_reduce_fusion.7, f32[12480]{0:T(1024)S(1)} %concatenate.32), channel_id=1, replica_groups=mesh['dp'=8,'tensor'=4] {'dp','tensor'}, use_global_device_ids=true, to_apply=%region_30.31 | all-reduce | flops 12481 | bytes 99848 | tf_op jit(solution)/shard_map/psum | solution.py:490
  1215.7 13.9 %add_multiply_fusion = (f32[1,1,235008]{2,1,0:T(1,128)}, f32[1,1,235008]{2,1,0:T(1,128)S(1)}, f32[1,1,235008]{2,1,0:T(1,128)}, f32[1,1,235008]{2,1,0:T(1,128)}) fusion(f32[1,1,235008]{2,1,0:T(1,128)} %param.29, f32[1,1,235008]{2,1,0:T(1,128)} %param.26, f32[1,1,235008]{2,1,0:T(1,128)} %param.27, f32[]{:T(128)S(6)} %div.105, ...), kind=kLoop, calls=%fused_computation.172 | loop fusion | flops 3995136 | bytes 9400328 | tf_op jit(solution)/shard_map/add | solution.py:261
  (558 shorter events, 255.5 us)
Async XLA Ops:
  7.2 120.5 %all-gather.8.cloned.1.call-start = ((), (), s32[]{:S(2)}) async-start(), calls=%async_computation.5 | async-start | bytes 8460288 | tf_op jit(solution)/shard_map/all_gather | solution.py:287
  9.8 234.3 %all-gather.6.cloned.1.call-start = ((), (), s32[]{:S(2)}) async-start(), calls=%async_computation.4 | async-start | bytes 3932160 | tf_op jit(solution)/shard_map/all_gather | solution.py:316
  10.2 350.0 %copy-start.92 = (pred[512]{0:T(512)(128)(4,1)}, pred[512]{0:T(512)(128)(4,1)S(1)}, u32[]{:S(2)}) copy-start(pred[512]{0:T(512)(128)(4,1)S(1)} %compare_reduce_fusion.1) | copy-start | bytes 1540
  10.8 351.5 %copy-start.64 = (f32[768]{0:T(1024)}, f32[768]{0:T(1024)S(1)}, u32[]{:S(2)}) copy-start(f32[768]{0:T(1024)S(1)} %get-tuple-element.399) | copy-start | bytes 9220
  12.3 347.9 %reduce-scatter.6.cloned.1.call-start = ((), (), s32[]{:S(2)}) async-start(), calls=%async_computation.6 | async-start | bytes 9830400 | tf_op jit(solution)/shard_map/reduce_scatter | solution.py:303
  13.2 183.9 %copy-start.87 = (f32[192]{0:T(256)}, f32[192]{0:T(256)S(1)}, u32[]{:S(2)}) copy-start(f32[192]{0:T(256)S(1)} %get-tuple-element.393) | copy-start | bytes 2308
  13.3 183.7 %copy-start.90 = (pred[512]{0:T(512)(128)(4,1)}, pred[512]{0:T(512)(128)(4,1)S(1)}, u32[]{:S(2)}) copy-start(pred[512]{0:T(512)(128)(4,1)S(1)} %compare_reduce_fusion) | copy-start | bytes 1540
  23.5 218.8 %copy-start.1 = (bf16[4,512,192]{1,2,0:T(8,128)(2,1)}, bf16[4,512,192]{1,2,0:T(8,128)(2,1)S(1)}, u32[]{:S(2)}) copy-start(bf16[4,512,192]{1,2,0:T(8,128)(2,1)S(1)} %all_gather.29) | copy-start | bytes 2359300
  292.8 99.6 %all-gather.10.cloned.1.call-start = ((), (), s32[]{:S(2)}) async-start(), calls=%async_computation.7 | async-start | bytes 3932160 | tf_op jit(solution)/shard_map/all_gather | solution.py:351
  363.7 128.8 %reduce-scatter.8.cloned.1.call-start = ((), (), s32[]{:S(2)}) async-start(), calls=%async_computation.8 | async-start | bytes 9830400 | tf_op jit(solution)/shard_map/reduce_scatter | solution.py:303
  365.8 15.8 %copy-start.57 = (f32[512]{0:T(512)}, f32[512]{0:T(512)S(1)}, u32[]{:S(2)}) copy-start(f32[512]{0:T(512)S(1)} %add_rsqrt_fusion.2) | copy-start | bytes 6148
  381.6 17.3 %copy-start.14 = (bf16[4,512,192]{1,2,0:T(8,128)(2,1)}, bf16[4,512,192]{1,2,0:T(8,128)(2,1)S(1)}, u32[]{:S(2)}) copy-start(bf16[4,512,192]{1,2,0:T(8,128)(2,1)S(1)} %get-tuple-element.354) | copy-start | bytes 2359300
  398.9 15.4 %copy-start.16 = (f32[4,512,768]{2,1,0:T(8,128)}, f32[4,512,768]{2,1,0:T(8,128)S(1)}, u32[]{:S(2)}) copy-start(f32[4,512,768]{2,1,0:T(8,128)S(1)} %get-tuple-element.406) | copy-start | bytes 18874372
  423.4 105.7 %all-gather.12.cloned.1.call-start = ((), (), s32[]{:S(2)}) async-start(), calls=%async_computation.9 | async-start | bytes 3932160 | tf_op jit(solution)/shard_map/all_gather | solution.py:378
  499.5 119.9 %reduce-scatter.10.cloned.1.call-start = ((), (), s32[]{:S(2)}) async-start(), calls=%async_computation.10 | async-start | bytes 9830400 | tf_op jit(solution)/shard_map/reduce_scatter | solution.py:303
  499.6 13.5 %copy-start.40 = (f32[4,512,192]{1,2,0:T(8,128)S(1)}, f32[4,512,192]{1,2,0:T(8,128)}, u32[]{:S(2)}) copy-start(f32[4,512,192]{1,2,0:T(8,128)} %copy-done.39) | copy-start | bytes 4718596
  499.6 13.5 %copy-start.41 = (f32[4,512,192]{1,2,0:T(8,128)S(1)}, f32[4,512,192]{1,2,0:T(8,128)}, u32[]{:S(2)}) copy-start(f32[4,512,192]{1,2,0:T(8,128)} %get-tuple-element.355) | copy-start | bytes 4718596
  501.0 12.1 copy-start.59
  501.1 12.0 copy-start.65
  502.2 10.9 copy-start.70
  502.2 10.9 copy-start.72
  549.9 116.7 %all-gather.14.cloned.1.call-start = ((), (), s32[]{:S(2)}) async-start(), calls=%async_computation.11 | async-start | bytes 3932160 | tf_op jit(solution)/shard_map/all_gather | solution.py:399
  627.0 468.1 %all-reduce.4.cloned.1.call-start = ((), (), s32[]{:S(2)}) async-start(), calls=%async_computation.13 | async-start | bytes 15040512
  651.9 12.0 copy-start.37
  666.6 8.9 copy-start.105
  677.7 7.7 copy-start
  819.3 13.2 %copy-start.9 = (f32[589824]{0:T(1024)S(1)}, f32[589824]{0:T(1024)}, u32[]{:S(2)}) copy-start(f32[589824]{0:T(1024)} %reshape.504) | copy-start | bytes 7077892
  847.9 317.9 %reduce-scatter.12.cloned.1.call-start = ((), (), s32[]{:S(2)}) async-start(), calls=%async_computation.12 | async-start | bytes 9830400 | tf_op jit(solution)/shard_map/reduce_scatter | solution.py:303
  864.0 8.8 copy-start.103
  864.0 9.5 copy-start.100
  869.0 298.7 %copy-start.17 = (f32[1,512,768]{1,2,0:T(8,128)S(1)}, f32[1,512,768]{1,2,0:T(8,128)}, u32[]{:S(2)}) copy-start(f32[1,512,768]{1,2,0:T(8,128)} %get-tuple-element.344) | copy-start | bytes 4718596
  874.2 293.5 %copy-start.85 = (f32[768]{0:T(1024)}, f32[768]{0:T(1024)S(1)}, u32[]{:S(2)}) copy-start(f32[768]{0:T(1024)S(1)} %dynamic_update_slice.48) | copy-start | bytes 9220
  1100.5 69.1 %copy-start.77 = (f32[768]{0:T(1024)S(1)}, f32[768]{0:T(1024)}, u32[]{:S(2)}) copy-start(f32[768]{0:T(1024)} %get-tuple-element.254) | copy-start | bytes 9220
  1100.5 69.1 %copy-start.78 = (f32[768]{0:T(1024)S(1)}, f32[768]{0:T(1024)}, u32[]{:S(2)}) copy-start(f32[768]{0:T(1024)} %get-tuple-element.255) | copy-start | bytes 9220
  1100.5 69.1 %copy-start.79 = (f32[768]{0:T(1024)S(1)}, f32[768]{0:T(1024)}, u32[]{:S(2)}) copy-start(f32[768]{0:T(1024)} %get-tuple-element.266) | copy-start | bytes 9220
  1100.5 69.1 %copy-start.80 = (f32[768]{0:T(1024)S(1)}, f32[768]{0:T(1024)}, u32[]{:S(2)}) copy-start(f32[768]{0:T(1024)} %get-tuple-element.372) | copy-start | bytes 9220
  1100.5 69.1 %copy-start.81 = (f32[768]{0:T(1024)S(1)}, f32[768]{0:T(1024)}, u32[]{:S(2)}) copy-start(f32[768]{0:T(1024)} %get-tuple-element.375) | copy-start | bytes 9220
  1100.5 69.1 %copy-start.84 = (f32[768]{0:T(1024)S(1)}, f32[768]{0:T(1024)}, u32[]{:S(2)}) copy-start(f32[768]{0:T(1024)} %copy-done.83) | copy-start | bytes 9220
  1100.6 69.1 %copy-start.93 = (f32[192]{0:T(256)S(1)}, f32[192]{0:T(256)}, u32[]{:S(2)}) copy-start(f32[192]{0:T(256)} %get-tuple-element.267) | copy-start | bytes 2308
  1100.6 69.1 %copy-start.94 = (f32[192]{0:T(256)S(1)}, f32[192]{0:T(256)}, u32[]{:S(2)}) copy-start(f32[192]{0:T(256)} %get-tuple-element.268) | copy-start | bytes 2308
  1100.6 69.1 %copy-start.95 = (f32[192]{0:T(256)S(1)}, f32[192]{0:T(256)}, u32[]{:S(2)}) copy-start(f32[192]{0:T(256)} %get-tuple-element.275) | copy-start | bytes 2308
  1100.6 69.1 %copy-start.96 = (f32[192]{0:T(256)S(1)}, f32[192]{0:T(256)}, u32[]{:S(2)}) copy-start(f32[192]{0:T(256)} %get-tuple-element.379) | copy-start | bytes 2308
  1100.6 69.1 %copy-start.97 = (f32[192]{0:T(256)S(1)}, f32[192]{0:T(256)}, u32[]{:S(2)}) copy-start(f32[192]{0:T(256)} %get-tuple-element.382) | copy-start | bytes 2308
  1167.7 46.6 %copy-start.49 = (f32[12480]{0:T(1024)S(1)}, f32[12480]{0:T(1024)}, u32[]{:S(2)}) copy-start(f32[12480]{0:T(1024)} %param.30) | copy-start | bytes 149764
  1167.7 46.6 %copy-start.54 = (f32[12480]{0:T(1024)S(1)}, f32[12480]{0:T(1024)}, u32[]{:S(2)}) copy-start(f32[12480]{0:T(1024)} %param.33) | copy-start | bytes 149764
  1167.7 46.6 %copy-start.55 = (f32[12480]{0:T(1024)S(1)}, f32[12480]{0:T(1024)}, u32[]{:S(2)}) copy-start(f32[12480]{0:T(1024)} %param.31) | copy-start | bytes 149764
  1167.7 46.6 %copy-start.56 = (f32[12480]{0:T(1024)S(1)}, f32[12480]{0:T(1024)}, u32[]{:S(2)}) copy-start(f32[12480]{0:T(1024)} %param.32) | copy-start | bytes 149764
  1215.1 14.5 %copy-start.50 = (f32[12480]{0:T(1024)}, f32[12480]{0:T(1024)S(1)}, u32[]{:S(2)}) copy-start(f32[12480]{0:T(1024)S(1)} %get-tuple-element.335) | copy-start | bytes 149764
  (79 other events, 256.7 us)
Sparse Core Ops, SparseCore 0:
  10.8 116.8 all-gather.7
  129.9 26.7 all-gather.5
  292.9 67.1 reduce-scatter.5
  363.9 28.5 all-gather.9
  423.5 68.9 reduce-scatter.7
  499.6 29.3 all-gather.11
  550.1 69.3 reduce-scatter.9
  627.1 28.5 all-gather.13
  848.0 247.0 all-reduce.3
  1097.7 68.0 reduce-scatter.11
where the time goes:
time: 1250 us; the launch traced here: 1240 us
  waiting for transfers between devices  610 us (49%)
  matrix products  183 us (15%)
  local copies, waits for them, and re-layouts  180 us (14%)
  other arithmetic  171 us (14%)
  blocking collectives  76.6 us (6%)
  between operations  18.3 us (1%)
    reduce_scatter x4, waiting for transfers between devices, head_total(): lax.psum_scatter(term_fn(jnp.int32(0), own_pages * lax.axis_size('tensor'...  267 us
    unnamed x11, waiting for transfers between devices  220 us
    all_gather x1, waiting for transfers between devices, shards(): gathered = lax.all_gather(wire, 'dp', axis=1, tiled=True)  104 us
    all_gather x1, other arithmetic, shards(): gathered = lax.all_gather(wire, 'dp', axis=1, tiled=True)  69.3 us
    dynamic_slice x56, local copies, waits for them, and re-layouts, shards(): lax.map(attend_page, (text_query, text_key, text_value, layout_query, lay...  44.4 us
    unnamed x234, local copies, waits for them, and re-layouts  43.8 us
    psum x1, blocking collectives, shards(): matrix_square = lax.psum(local_square, ('dp', 'tensor'))  40.2 us
    dot_general x12, matrix products, project_back(): jnp.einsum('pse,de->psd', incoming, weight, preferred_element_type=jnp.fl...  35.4 us
  transfers between devices with their start and end apart: 10, of which 8 were waited for; matrix products, arithmetic and copies ran while one was open for 16% of the time, Pallas kernels for 0%

commit v1 on v0

v1 whole, which is shorter than its diff:
```python
from functools import partial
import math

import jax
import jax.numpy as jnp
from jax import lax
from jax.experimental import pallas as pl
from jax.experimental.pallas import tpu as pltpu
from jax.sharding import PartitionSpec as P

D = 768
HT = 64
FF = 3072
L = 192
HL = 16
LF = 768
STEP = 5


norm_eps = 1e-05
clip_bound = 1.0
first_decay = 0.5
second_decay = 0.6
adam_floor = 1e-08
weight_decay = 0.01
vector_rate = 0.5
average_keep = 0.5
masked_score = -1e30


def piece_table(parts):
    text_spread = 1.0 / math.sqrt(D)
    layout_spread = 1.0 / math.sqrt(L)
    return [
        (D, D // parts, text_spread),
        (D, D // parts, text_spread),
        (D, D // parts, text_spread),
        (D // parts, D, 8.0 * text_spread),
        (D, FF // parts, text_spread),
        (FF // parts, D, 1.0 / math.sqrt(FF)),
        (L, L // parts, layout_spread),
        (L, L // parts, layout_spread),
        (L, L // parts, layout_spread),
        (L // parts, L, 8.0 * layout_spread),
        (L, LF // parts, layout_spread),
        (LF // parts, L, 1.0 / math.sqrt(LF)),
    ]


def rate_table(parts):
    return jnp.concatenate(
        [
            jnp.full((height * width,), spread, jnp.float32)
            for height, width, spread in piece_table(parts)
        ]
    )


def split_vector(flat):
    pieces = []
    start = 0
    for width in [D] * 8 + [FF] + [L] * 8 + [LF] + [D, L]:
        pieces.append(flat[start : start + width])
        start = start + width
    return pieces


def project(acts, weight):
    return jnp.einsum("psd,de->pse", acts, weight, preferred_element_type=jnp.float32)


def project_back(incoming, weight):
    return jnp.einsum("pse,de->psd", incoming, weight, preferred_element_type=jnp.float32)


def weight_grad(acts, incoming):
    return jnp.einsum("psd,pse->de", acts, incoming, preferred_element_type=jnp.float32)


def norm_forward(value, gain, shift):
    mean = jnp.mean(value, -1, keepdims=True)
    centred = value - mean
    scale = lax.rsqrt(jnp.mean(centred * centred, -1, keepdims=True) + norm_eps)
    normed = centred * scale
    return (normed * gain + shift, normed, scale)


def norm_backward(incoming, normed, scale, gain):
    scaled = incoming * gain
    result = scale * (
        scaled
        - jnp.mean(scaled, -1, keepdims=True)
        - normed * jnp.mean(scaled * normed, -1, keepdims=True)
    )
    return (result, jnp.sum(incoming * normed, (0, 1)), jnp.sum(incoming, (0, 1)))


def gelu_back(value, incoming):
    unused, pull = jax.vjp(partial(jax.nn.gelu, approximate=False), value)
    return pull(incoming)[0]


def adam_update(weight, gradient, first, second, average, rate, factor):
    clipped = gradient * factor
    new_first = first_decay * first + (1.0 - first_decay) * clipped
    new_second = second_decay * second + (1.0 - second_decay) * clipped * clipped
    first_hat = new_first / (1.0 - first_decay**STEP)
    second_hat = new_second / (1.0 - second_decay**STEP)
    updated = weight - rate * (
        first_hat / (jnp.sqrt(second_hat) + adam_floor) + weight_decay * weight
    )
    return (
        updated,
        new_first,
        new_second,
        updated.astype(jnp.bfloat16),
        average_keep * average + (1.0 - average_keep) * updated,
    )


NT = (((1,), (1,)), ((), ()))
NN = (((1,), (0,)), ((), ()))
TN = (((0,), (0,)), ((), ()))


def dot(left, right, dims):
    return lax.dot_general(left, right, dims, preferred_element_type=jnp.float32)


def lane_of(shape):
    return lax.broadcasted_iota(jnp.int32, shape, len(shape) - 1)


def head_tiles(text_ref, layout_ref, slot, tile, high):
    first = slot * 256 + tile * 128
    text = text_ref[0, :, first : first + 128]
    layout = layout_ref[0, :, first : first + 128]
    low = lane_of(text.shape) < 64
    if high:
        return jnp.where(low, layout, text)
    return jnp.where(low, text, layout)


def own_lanes(shape, high):
    low = lane_of(shape) < 64
    return ~low if high else low


def scaled_query(query, high):
    own = own_lanes(query.shape, high)
    marker = 16 if high else 80
    scale = jnp.where(own, 0.125, 0.25)
    scaled = (query.astype(jnp.float32) * scale).astype(jnp.bfloat16)
    return jnp.where(lane_of(query.shape) == marker, jnp.bfloat16(1.0), scaled)


def masked_key(key, high, length):
    marker = 16 if high else 80
    beyond = lax.broadcasted_iota(jnp.int32, key.shape, 0) >= length
    column = jnp.where(beyond, jnp.float32(-1e30), jnp.float32(0.0)).astype(jnp.bfloat16)
    return jnp.where(lane_of(key.shape) == marker, column, key)


def attend_kernel(length_ref, text_ref, layout_ref, context_ref, layout_context_ref, total_ref):
    length = length_ref[0]
    found = []
    for head in range(3):
        tile, high = head // 2, head % 2 == 1
        query = scaled_query(head_tiles(text_ref, layout_ref, 0, tile, high), high)
        key = masked_key(head_tiles(text_ref, layout_ref, 1, tile, high), high, length)
        value = head_tiles(text_ref, layout_ref, 2, tile, high)
        scores = dot(key, query, NT)
        top = jnp.max(scores, 0, keepdims=True)
        raised = jnp.exp(scores - top)
        total = jnp.sum(raised, 0, keepdims=True)
        probs = (raised * (1.0 / total)).astype(jnp.bfloat16)
        total_ref[0, head : head + 1, :] = top + jnp.log(total)
        context = dot(value, probs, TN)
        found.append(context.T)
    low = lane_of(found[0].shape) < 64
    zero = jnp.zeros_like(found[0])
    context_ref[0, :, 0:128] = jnp.where(low, found[0], found[1]).astype(jnp.bfloat16)
    context_ref[0, :, 128:256] = jnp.where(low, found[2], zero).astype(jnp.bfloat16)
    layout_context_ref[0, :, 0:128] = jnp.where(low, found[1], found[0]).astype(jnp.bfloat16)
    layout_context_ref[0, :, 128:256] = jnp.where(low, zero, found[2]).astype(jnp.bfloat16)


def block(rows, width):
    return pl.BlockSpec((1, rows, width), lambda t: (t, 0, 0))


def attend(length, text, layout):
    parts, positions, _ = text.shape
    return pl.pallas_call(
        attend_kernel,
        grid=(parts,),
        in_specs=[
            pl.BlockSpec(memory_space=pltpu.SMEM),
            block(positions, 768),
            block(positions, 768),
        ],
        out_specs=[block(positions, 256), block(positions, 256), block(8, positions)],
        out_shape=[
            jax.ShapeDtypeStruct((parts, positions, 256), jnp.bfloat16),
            jax.ShapeDtypeStruct((parts, positions, 256), jnp.bfloat16),
            jax.ShapeDtypeStruct((parts, 8, positions), jnp.float32),
        ],
        compiler_params=pltpu.CompilerParams(vmem_limit_bytes=40 << 20),
        cost_estimate=pl.CostEstimate(flops=3 << 30, transcendentals=3 << 20, bytes_accessed=10 << 20),
        name="attend",
    )(length, text, layout)


def attend_back_kernel(
    length_ref,
    text_ref,
    layout_ref,
    total_ref,
    context_ref,
    layout_context_ref,
    context_grad_ref,
    layout_context_grad_ref,
    text_grad_ref,
    layout_grad_ref,
):
    length = length_ref[0]
    grads = ([], [], [])
    for head in range(3):
        tile, high = head // 2, head % 2 == 1
        raw_query = head_tiles(text_ref, layout_ref, 0, tile, high)
        raw_key = head_tiles(text_ref, layout_ref, 1, tile, high)
        value = head_tiles(text_ref, layout_ref, 2, tile, high)
        incoming = head_tiles(context_grad_ref, layout_context_grad_ref, 0, tile, high)
        context = head_tiles(context_ref, layout_context_ref, 0, tile, high)
        own = own_lanes(value.shape, high)
        query = scaled_query(raw_query, high)
        key = masked_key(raw_key, high, length)
        product = (incoming.astype(jnp.float32) * context.astype(jnp.float32)).T
        start = 0 if high else 64
        layout_mean = jnp.sum(product[start : start + 16], 0, keepdims=True)
        joint_mean = jnp.sum(product, 0, keepdims=True)
        zero = jnp.zeros_like(value)
        probs = jnp.exp(dot(key, query, NT) - total_ref[0, head : head + 1, :])
        value_grad = dot(probs.astype(jnp.bfloat16), incoming, NN)
        joint = (probs * (dot(value, incoming, NT) - joint_mean)).astype(jnp.bfloat16)
        alone = (
            probs * (dot(jnp.where(own, zero, value), incoming, NT) - layout_mean)
        ).astype(jnp.bfloat16)
        key_grad = jnp.where(own, dot(joint, raw_query, NN) * 0.125, dot(alone, raw_query, NN) * 0.25)
        rows = lax.broadcasted_iota(jnp.int32, (128, value.shape[0]), 0) < 64
        if high:
            rows = ~rows
        query_grad = jnp.where(
            rows, dot(raw_key, joint, TN) * 0.125, dot(raw_key, alone, TN) * 0.25
        )
        grads[0].append(query_grad.T)
        grads[1].append(key_grad)
        grads[2].append(value_grad)
    low = lane_of(grads[0][0].shape) < 64
    zero = jnp.zeros_like(grads[0][0])
    for slot in range(3):
        first, second, third = grads[slot]
        at = slot * 256
        text_grad_ref[0, :, at : at + 128] = jnp.where(low, first, second).astype(jnp.bfloat16)
        text_grad_ref[0, :, at + 128 : at + 256] = jnp.where(low, third, zero).astype(jnp.bfloat16)
        layout_grad_ref[0, :, at : at + 128] = jnp.where(low, second, first).astype(jnp.bfloat16)
        layout_grad_ref[0, :, at + 128 : at + 256] = jnp.where(low, zero, third).astype(
            jnp.bfloat16
        )


def attend_back(length, text, layout, total, context, layout_context, grad, layout_grad):
    parts, positions, _ = text.shape
    return pl.pallas_call(
        attend_back_kernel,
        grid=(parts,),
        in_specs=[
            pl.BlockSpec(memory_space=pltpu.SMEM),
            block(positions, 768),
            block(positions, 768),
            block(8, positions),
            block(positions, 256),
            block(positions, 256),
            block(positions, 256),
            block(positions, 256),
        ],
        out_specs=[block(positions, 768), block(positions, 768)],
        out_shape=[
            jax.ShapeDtypeStruct((parts, positions, 768), jnp.bfloat16),
            jax.ShapeDtypeStruct((parts, positions, 768), jnp.bfloat16),
        ],
        compiler_params=pltpu.CompilerParams(vmem_limit_bytes=40 << 20),
        cost_estimate=pl.CostEstimate(flops=12 << 30, transcendentals=3 << 20, bytes_accessed=20 << 20),
        name="attend_back",
    )(length, text, layout, total, context, layout_context, grad, layout_grad)


SPAN = 235008
FRAME = 320
UNIT = 768


def cast_kernel(shift_ref, master_ref, frame_ref, flat_ref):
    whole = SPAN // 1024
    for step in range(whole):
        flat_ref[pl.ds(8 * step, 8), :] = master_ref[0, 0, pl.ds(1024 * step, 1024)].reshape(8, 128)
    flat_ref[pl.ds(8 * whole, 4), :] = master_ref[0, 0, pl.ds(1024 * whole, 512)].reshape(4, 128)
    for column in range(6):
        rows = flat_ref[pl.ds(column, 306, stride=6), :]
        rows = jnp.concatenate((rows, jnp.zeros((14, 128), jnp.float32)), 0)
        rows = pltpu.roll(rows, shift_ref[0], 0)
        frame_ref[0, :, column * 128 : column * 128 + 128] = rows.astype(jnp.bfloat16)


def cast_frame(shift, master):
    return pl.pallas_call(
        cast_kernel,
        in_specs=[pl.BlockSpec(memory_space=pltpu.SMEM), pl.BlockSpec(memory_space=pltpu.VMEM)],
        out_specs=pl.BlockSpec(memory_space=pltpu.VMEM),
        out_shape=jax.ShapeDtypeStruct((1, FRAME, UNIT), jnp.bfloat16),
        scratch_shapes=[pltpu.VMEM((1840, 128), jnp.float32)],
        name="cast_frame",
    )(shift, master)


def finish_kernel(shift_ref, keep_ref, other_ref, flat_out_ref, square_ref, flat_ref):
    squares = jnp.zeros((8, 128), jnp.float32)
    for column in range(6):
        at = column * 128
        rows = keep_ref[:, at : at + 128].astype(jnp.float32)
        rows = rows + other_ref[:, at : at + 128].astype(jnp.float32)
        rows = pltpu.roll(rows, FRAME - shift_ref[0], 0)
        flat_ref[pl.ds(column, 306, stride=6), :] = rows[:306]
        inside = lax.broadcasted_iota(jnp.int32, rows.shape, 0) < 306
        masked = jnp.where(inside, rows, 0.0)
        squares = squares + jnp.sum((masked * masked).reshape(40, 8, 128), 0)
    square_ref[...] = squares
    whole = SPAN // 1024
    for step in range(whole):
        flat_out_ref[0, 0, pl.ds(1024 * step, 1024)] = flat_ref[pl.ds(8 * step, 8), :].reshape(1024)
    flat_out_ref[0, 0, pl.ds(1024 * whole, 512)] = flat_ref[pl.ds(8 * whole, 4), :].reshape(512)


def finish(shift, keep, other):
    return pl.pallas_call(
        finish_kernel,
        in_specs=[pl.BlockSpec(memory_space=pltpu.SMEM)]
        + [pl.BlockSpec(memory_space=pltpu.VMEM)] * 2,
        out_specs=[pl.BlockSpec(memory_space=pltpu.VMEM)] * 2,
        out_shape=[
            jax.ShapeDtypeStruct((1, 1, SPAN), jnp.float32),
            jax.ShapeDtypeStruct((8, 128), jnp.float32),
        ],
        scratch_shapes=[pltpu.VMEM((1840, 128), jnp.float32)],
        name="finish",
    )(shift, keep, other)


RATE_STEPS = (
    (0, 768.0**-0.5),
    (576, 8.0 * 768.0**-0.5),
    (768, 768.0**-0.5),
    (1536, 3072.0**-0.5),
    (2304, 192.0**-0.5),
    (2340, 8.0 * 192.0**-0.5),
    (2352, 192.0**-0.5),
    (2400, 768.0**-0.5),
)


def adam_kernel(
    first_index_ref,
    factor_ref,
    weight_ref,
    gradient_ref,
    first_ref,
    second_ref,
    average_ref,
    new_weight_ref,
    new_first_ref,
    new_second_ref,
    low_ref,
    new_average_ref,
):
    width = weight_ref.shape[2]
    start = first_index_ref[0] + pl.program_id(0) * width
    factor = factor_ref[0]
    for at in range(0, width, CHUNK):
        count = min(CHUNK, width - at)
        place = pl.ds(at, count)

        def load(ref):
            return ref[0, 0, place].reshape(count // 128, 128)

        def store(ref, value):
            ref[0, 0, place] = value.reshape(count)

        shape = (count // 128, 128)
        index = lax.broadcasted_iota(jnp.int32, shape, 0) * 128 + start + at
        rate = jnp.full(shape, RATE_STEPS[0][1], jnp.float32)
        for row, value in RATE_STEPS[1:]:
            rate = jnp.where(index >= row * UNIT, jnp.float32(value), rate)
        weight = load(weight_ref)
        clipped = load(gradient_ref) * factor
        new_first = 0.5 * load(first_ref) + 0.5 * clipped
        new_second = 0.6 * load(second_ref) + 0.4 * clipped * clipped
        first_hat = new_first * (1.0 / (1.0 - 0.5**5))
        second_hat = new_second * (1.0 / (1.0 - 0.6**5))
        updated = weight - rate * (first_hat / (jnp.sqrt(second_hat) + 1e-8) + 0.01 * weight)
        store(new_weight_ref, updated)
        store(new_first_ref, new_first)
        store(new_second_ref, new_second)
        low_ref[0, 0, place] = updated.reshape(count).astype(jnp.bfloat16)
        store(new_average_ref, 0.5 * load(average_ref) + 0.5 * updated)


CHUNK = 1024


def adam(first_index, factor, weight, gradient, first, second, average, steps=3):
    span = weight.shape[2]
    spec = pl.BlockSpec((1, 1, span // steps), lambda i: (0, 0, i))
    full = jax.ShapeDtypeStruct(weight.shape, jnp.float32)
    return pl.pallas_call(
        adam_kernel,
        grid=(steps,),
        in_specs=[pl.BlockSpec(memory_space=pltpu.SMEM)] * 2 + [spec] * 5,
        out_specs=[spec] * 5,
        out_shape=[full, full, full, jax.ShapeDtypeStruct(weight.shape, jnp.bfloat16), full],
        name="adam",
    )(first_index, factor, weight, gradient, first, second, average)


def placing(rows, columns, row_axis):
    narrow = lax.broadcasted_iota(jnp.int32, (rows, columns), row_axis)
    wide = lax.broadcasted_iota(jnp.int32, (rows, columns), 1 - row_axis)
    place = jnp.where(narrow < 16, narrow + 64, jnp.where(narrow < 32, narrow - 16, narrow + 160))
    return jnp.where(place == wide, 1.0, 0.0).astype(jnp.bfloat16)


def wide_rows(value):
    return jnp.concatenate((value, jnp.zeros((value.shape[0], 64), value.dtype)), 1)


def unpack_kernel(
    heads_ref, out_ref, small_ref, qkv_ref, wo_ref, lqkv_ref, lwo_ref, lw1_ref, lw2_ref, rows_ref, small_rows_ref
):
    def spread(source_ref, first, count, stride, target_ref):
        for step in range(4):
            piece = wide_rows(source_ref[first : first + count, 192 * step : 192 * step + 192])
            target_ref[0, pl.ds(step, count, stride=stride), :] = piece[:, :128]
            target_ref[1, pl.ds(step, count, stride=stride), :] = piece[:, 128:]

    small_rows_ref[...] = small_ref[0].astype(jnp.float32)
    for slot in range(3):
        for step in range(4):
            piece = heads_ref[0, 192 * slot : 192 * slot + 192, 192 * step : 192 * step + 192]
            piece = wide_rows(piece.astype(jnp.float32))
            rows_ref[0, pl.ds(step, 192, stride=4), :] = piece[:, :128]
            rows_ref[1, pl.ds(step, 192, stride=4), :] = piece[:, 128:]
        qkv_ref[0, :, 256 * slot : 256 * slot + 128] = rows_ref[0].astype(jnp.bfloat16)
        qkv_ref[0, :, 256 * slot + 128 : 256 * slot + 256] = rows_ref[1].astype(jnp.bfloat16)
    wo_ref[0, :192, :] = out_ref[0]
    wo_ref[0, 192:, :] = jnp.zeros((64, 768), jnp.bfloat16)
    place = placing(48, 256, 0)
    narrow = jnp.concatenate(
        [small_rows_ref[0:48, 48 * step : 48 * step + 48] for step in range(16)], 0
    )
    placed = dot(narrow.astype(jnp.bfloat16), place, NN)
    for slot in range(3):
        for step in range(16):
            piece = placed[48 * step + 12 * slot : 48 * step + 12 * slot + 12]
            rows_ref[0, pl.ds(step, 12, stride=16), :] = piece[:, :128]
            rows_ref[1, pl.ds(step, 12, stride=16), :] = piece[:, 128:]
        lqkv_ref[0, :, 256 * slot : 256 * slot + 128] = rows_ref[0, 0:192].astype(jnp.bfloat16)
        lqkv_ref[0, :, 256 * slot + 128 : 256 * slot + 256] = rows_ref[1, 0:192].astype(jnp.bfloat16)
    spread(small_rows_ref, 36, 12, 4, rows_ref)
    lwo_ref[...] = jnp.zeros_like(lwo_ref)
    for head, at in enumerate((64, 0, 192)):
        for half, width in ((0, 128), (1, 64)):
            lwo_ref[0, at : at + 16, 128 * half : 128 * half + width] = rows_ref[
                half, 16 * head : 16 * head + 16, :width
            ].astype(jnp.bfloat16)
    for first, target_ref in ((48, lw1_ref), (96, lw2_ref)):
        spread(small_rows_ref, first, 48, 4, rows_ref)
        target_ref[0, :, 0:128] = rows_ref[0, 0:192].astype(jnp.bfloat16)
        target_ref[0, :, 128:192] = rows_ref[1, 0:192, :64].astype(jnp.bfloat16)


def unpack(stack):
    parts = stack.shape[0]

    def spec(rows, width, at=0):
        return pl.BlockSpec((1, rows, width), lambda t: (t, at, 0))

    shapes = ((768, 768), (256, 768), (192, 768), (256, 192), (192, 192), (192, 192))
    return pl.pallas_call(
        unpack_kernel,
        grid=(parts,),
        in_specs=[spec(576, 768), spec(192, 768, 3), spec(144, 768, 16)],
        out_specs=[spec(*shape) for shape in shapes],
        out_shape=[jax.ShapeDtypeStruct((parts,) + shape, jnp.bfloat16) for shape in shapes],
        scratch_shapes=[pltpu.VMEM((2, 768, 128), jnp.float32), pltpu.VMEM((144, 768), jnp.float32)],
        compiler_params=pltpu.CompilerParams(vmem_limit_bytes=40 << 20),
        name="unpack",
    )(stack, stack, stack)


def pack_kernel(qkv_ref, lqkv_ref, lwo_ref, lw1_ref, lw2_ref, heads_ref, small_ref, slots_ref, small_rows_ref, rows_ref):
    for slot in range(3):
        for half in range(2):
            at = 256 * slot + 128 * half
            rows_ref[half] = qkv_ref[0, :, at : at + 128]
        for step in range(4):
            piece = jnp.concatenate(
                [rows_ref[half, pl.ds(step, 192, stride=4), :] for half in range(2)], 1
            )
            heads_ref[0, 192 * slot : 192 * slot + 192, 192 * step : 192 * step + 192] = piece[
                :, :192
            ].astype(jnp.bfloat16)
    slots_ref[...] = jnp.zeros_like(slots_ref)
    for slot in range(3):
        for half in range(2):
            at = 256 * slot + 128 * half
            rows_ref[half, 0:192] = lqkv_ref[0, :, at : at + 128]
            for step in range(16):
                row = 16 * (3 * step + slot)
                slots_ref[row : row + 12, 128 * half : 128 * half + 128] = rows_ref[
                    half, pl.ds(step, 12, stride=16), :
                ]
    placed = dot(slots_ref[...].astype(jnp.bfloat16), placing(256, 48, 1), NN)
    for slot in range(3):
        for step in range(16):
            at = 16 * (3 * step + slot)
            small_rows_ref[12 * slot : 12 * slot + 12, 48 * step : 48 * step + 48] = placed[at : at + 12]

    def gather(first, count):
        for step in range(4):
            piece = jnp.concatenate([rows_ref[half, pl.ds(step, count, stride=4), :] for half in range(2)], 1)
            small_rows_ref[first : first + count, 192 * step : 192 * step + 192] = piece[:, :192]

    for head, at in enumerate((64, 0, 192)):
        rows_ref[0, 16 * head : 16 * head + 16, :] = lwo_ref[0, at : at + 16, 0:128]
        rows_ref[1, 16 * head : 16 * head + 16, 0:64] = lwo_ref[0, at : at + 16, 128:192]
    gather(36, 12)
    for first, source_ref in ((48, lw1_ref), (96, lw2_ref)):
        rows_ref[0, 0:192, :] = source_ref[0, :, 0:128]
        rows_ref[1, 0:192, 0:64] = source_ref[0, :, 128:192]
        gather(first, 48)
    small_ref[0] = small_rows_ref[...].astype(jnp.bfloat16)


def pack(qkv, lqkv, lwo, lw1, lw2):
    parts = qkv.shape[0]

    def spec(rows, width):
        return pl.BlockSpec((1, rows, width), lambda t: (t, 0, 0))

    return pl.pallas_call(
        pack_kernel,
        grid=(parts,),
        in_specs=[spec(*item.shape[1:]) for item in (qkv, lqkv, lwo, lw1, lw2)],
        out_specs=[spec(576, 768), spec(144, 768)],
        out_shape=[
            jax.ShapeDtypeStruct((parts, 576, 768), jnp.bfloat16),
            jax.ShapeDtypeStruct((parts, 144, 768), jnp.bfloat16),
        ],
        scratch_shapes=[
            pltpu.VMEM((768, 256), jnp.float32),
            pltpu.VMEM((144, 768), jnp.float32),
            pltpu.VMEM((2, 768, 128), jnp.float32),
        ],
        compiler_params=pltpu.CompilerParams(vmem_limit_bytes=40 << 20),
        name="pack",
    )(qkv, lqkv, lwo, lw1, lw2)


def exchange_pairs(flip):
    pairs = []
    for device in range(32):
        z, x, y, core = device // 8, device // 4 % 2, device // 2 % 2, device % 2
        z, x, y, core = flip(z, x, y, core)
        pairs.append((device, z * 8 + x * 4 + y * 2 + core))
    return pairs


ROUNDS = (
    exchange_pairs(lambda z, x, y, core: (z, x, y, 1 - core)),
    exchange_pairs(lambda z, x, y, core: (z, x, 1 - y, core) if core else (z, 1 - x, y, core)),
    exchange_pairs(lambda z, x, y, core: (z, 1 - x, y, core) if core else (z, x, 1 - y, core)),
    exchange_pairs(lambda z, x, y, core: (z ^ 1, x, y, core) if core else (z ^ 2, x, y, core)),
    exchange_pairs(lambda z, x, y, core: (z ^ 2, x, y, core) if core else (z ^ 1, x, y, core)),
)


def swap(value, step):
    return lax.ppermute(value, ("dp", "tensor"), ROUNDS[step])


def total_of(value):
    for step in range(5):
        value = value + swap(value, step)
    return value


def picked(value, index, axis):
    return lax.dynamic_index_in_dim(value, index, axis, keepdims=False)


def added(left, right):
    return (left.astype(jnp.float32) + right.astype(jnp.float32)).astype(jnp.bfloat16)


def core_stage(blocks, core):
    split = blocks.reshape((2, 2) + blocks.shape[1:])
    return picked(split, core, 1), swap(picked(split, 1 - core, 1), 0)


def plane_stages(kept, received, starts, place):
    z, x, y, core = place

    def window(part, across, k):
        at = jnp.where(across == 0, starts[0][k], starts[1][k])
        where = (part, at, 0, 0)
        size = (1, 20, 16, UNIT)
        return added(
            lax.dynamic_slice(kept, where, size), lax.dynamic_slice(received, where, size)
        )

    def side(other):
        rows = []
        for entry in range(2):
            own_x, own_y = (1 - x, 1 - y) if other else (x, y)
            part = jnp.where(core == 0, entry, own_y)
            across = jnp.where(core == 0, own_x, entry)
            rows.append(jnp.concatenate([window(part, across, k) for k in range(2)], 0))
        return jnp.stack(rows)

    second = added(side(False), swap(side(True), 1))
    own = jnp.where(core == 0, y, x)
    return added(picked(second, own, 0), swap(picked(second, 1 - own, 0), 2))


def line_stages(first, second, place):
    z, x, y, core = place
    blocks = jnp.concatenate((second, first), 0)
    order = jnp.where(x == 0, jnp.array([0, 1, 2, 3]), jnp.array([0, 2, 3, 1]))
    high, low = z // 2, z % 2
    lead = jnp.where(core == 0, high, low)
    rest = jnp.where(core == 0, low, high)

    def block(leading, trailing):
        layer = jnp.where(core == 0, 2 * leading + trailing, leading + 2 * trailing)
        return picked(blocks, order[layer], 0)

    kept = jnp.stack([block(lead, entry) for entry in range(2)])
    sent = jnp.stack([block(1 - lead, entry) for entry in range(2)])
    third = added(kept, swap(sent, 3))
    return picked(third, rest, 0), swap(picked(third, 1 - rest, 0), 4)


def spaced(vector):
    gap = jnp.zeros((4, 48), vector.dtype)
    first, second, third = vector[:, 0:16], vector[:, 16:32], vector[:, 32:48]
    return jnp.concatenate((second, gap, first, gap, gap, gap[:, :16], third, gap), 1)


def unspaced(value):
    return jnp.concatenate((value[:, 64:80], value[:, 0:16], value[:, 192:208]), 1).reshape(-1)


def shards(
    text_in,
    layout_in,
    lengths,
    text_mask,
    box_mask,
    text_cot,
    layout_cot,
    master,
    first_moment,
    second_moment,
    ema_weights,
    vectors,
    vector_first,
    vector_second,
    vector_ema,
):
    parts = lax.axis_size("tensor")
    dp_count = lax.axis_size("dp")
    tensor_index = lax.axis_index("tensor")
    dp_index = lax.axis_index("dp")
    span = master.shape[2]
    near = dp_count == 8 and parts == 4
    place = (dp_index // 2, dp_index % 2, tensor_index // 2, tensor_index % 2)
    shift = (2 * dp_index).reshape(1)
    if near:
        frame = cast_frame(shift, master)
        frames = lax.all_gather(frame, ("tensor", "dp"), axis=0, tiled=True)
        frames = frames.reshape(parts, dp_count, FRAME, UNIT)
        before = jnp.pad(frames[:, :-1, 304:], ((0, 0), (1, 0), (0, 0), (0, 0)))
        stack = jnp.concatenate((frames[:, :, :16] + before, frames[:, :, 16:304]), 2)
        stack = jnp.concatenate((stack.reshape(parts, -1, UNIT), frames[:, -1, 304:]), 1)
    else:
        wire = master.reshape(-1, 192).astype(jnp.bfloat16)
        stack = lax.all_gather(wire[None], ("tensor", "dp"), axis=0, tiled=True)
        stack = stack.reshape(parts, -1, UNIT)
    qkv_weight, out_weight, lqkv_weight, lout_weight, lup_weight, ldown_weight = unpack(stack)
    up_weight, down_weight = stack[:, 768:1536], stack[:, 1536:2304]
    biases = split_vector(vectors)
    length = lax.dynamic_slice_in_dim(lengths, tensor_index, 1)

    def product(spec, left, right):
        return jnp.einsum(spec, left, right, preferred_element_type=jnp.float32)

    def over_parts(spec, left, right):
        return sum(product(spec, left[part], right[part]) for part in range(parts))

    def summed(value):
        return jnp.sum(value, 0, dtype=jnp.float32)

    def backward_norm(incoming, normed, scale, gain):
        result, gain_grad, shift_grad = norm_backward(
            incoming[None], normed[None], scale[None], gain
        )
        return result[0], gain_grad, shift_grad

    gap = jnp.zeros((parts, 64), jnp.float32)
    none = jnp.zeros((parts, 256), jnp.float32)
    qkv_bias = jnp.concatenate(
        (biases[0].reshape(parts, 192), gap, none, biases[1].reshape(parts, 192), gap), 1
    )
    lqkv_bias = jnp.concatenate(
        (spaced(biases[9].reshape(parts, 48)), none, spaced(biases[10].reshape(parts, 48))), 1
    )
    text_flag = (text_mask[0] > 0)[:, None]
    box_flag = (box_mask[0] > 0)[:, None]
    text_act = jnp.where(text_flag, biases[18], text_in[0].astype(jnp.float32))
    layout_act = jnp.where(box_flag, biases[19], layout_in[0].astype(jnp.float32))
    text_low = text_act.astype(jnp.bfloat16)
    layout_low = layout_act.astype(jnp.bfloat16)
    qkv = (product("sd,tde->tse", text_low, qkv_weight) + qkv_bias[:, None]).astype(jnp.bfloat16)
    lqkv = (product("sd,tde->tse", layout_low, lqkv_weight) + lqkv_bias[:, None]).astype(
        jnp.bfloat16
    )
    context, lcontext, log_total = attend(length, qkv, lqkv)
    text_attn = over_parts("sc,cd->sd", context, out_weight)
    layout_attn = over_parts("sc,cd->sd", lcontext, lout_weight)
    text_mid, text_normed_one, text_scale_one = norm_forward(
        text_attn + biases[2] + text_act, biases[3], biases[4]
    )
    layout_mid, layout_normed_one, layout_scale_one = norm_forward(
        layout_attn + biases[11] + layout_act, biases[12], biases[13]
    )
    text_mid_low = text_mid.astype(jnp.bfloat16)
    layout_mid_low = layout_mid.astype(jnp.bfloat16)
    text_up = product("sd,tde->tse", text_mid_low, up_weight) + biases[8].reshape(parts, 1, -1)
    layout_up = product("sd,tde->tse", layout_mid_low, lup_weight) + biases[17].reshape(
        parts, 1, -1
    )
    text_hidden = jax.nn.gelu(text_up, approximate=False).astype(jnp.bfloat16)
    layout_hidden = jax.nn.gelu(layout_up, approximate=False).astype(jnp.bfloat16)
    text_down = over_parts("se,ed->sd", text_hidden, down_weight)
    layout_down = over_parts("se,ed->sd", layout_hidden, ldown_weight)
    text_final, text_normed_two, text_scale_two = norm_forward(
        text_down + biases[5] + text_mid, biases[6], biases[7]
    )
    layout_final, layout_normed_two, layout_scale_two = norm_forward(
        layout_down + biases[14] + layout_mid, biases[15], biases[16]
    )
    text_pre_two, text_gain_two, text_shift_two = backward_norm(
        text_cot[0].astype(jnp.float32), text_normed_two, text_scale_two, biases[6]
    )
    layout_pre_two, layout_gain_two, layout_shift_two = backward_norm(
        layout_cot[0].astype(jnp.float32), layout_normed_two, layout_scale_two, biases[15]
    )
    text_down_in = text_pre_two.astype(jnp.bfloat16)
    layout_down_in = layout_pre_two.astype(jnp.bfloat16)
    text_up_grad = gelu_back(text_up, product("sd,ted->tse", text_down_in, down_weight)).astype(
        jnp.bfloat16
    )
    layout_up_grad = gelu_back(
        layout_up, product("sd,ted->tse", layout_down_in, ldown_weight)
    ).astype(jnp.bfloat16)
    down_grad = product("tse,sd->ted", text_hidden, text_down_in).astype(jnp.bfloat16)
    ldown_grad = product("tse,sd->ted", layout_hidden, layout_down_in)
    up_grad = product("sd,tse->tde", text_mid_low, text_up_grad).astype(jnp.bfloat16)
    lup_grad = product("sd,tse->tde", layout_mid_low, layout_up_grad)
    if near:
        early = jnp.concatenate((up_grad[:, 144:], down_grad[:, :608]), 1)
        early = early.reshape(parts, 77, 16, UNIT)
        early_kept, early_received = core_stage(early, place[3])
        early_sum = plane_stages(early_kept, early_received, ((19, 57), (0, 38)), place)
    text_mid_back = over_parts("se,de->sd", text_up_grad, up_weight)
    layout_mid_back = over_parts("se,de->sd", layout_up_grad, lup_weight)
    text_pre_one, text_gain_one, text_shift_one = backward_norm(
        text_pre_two + text_mid_back, text_normed_one, text_scale_one, biases[3]
    )
    layout_pre_one, layout_gain_one, layout_shift_one = backward_norm(
        layout_pre_two + layout_mid_back, layout_normed_one, layout_scale_one, biases[12]
    )
    text_attn_in = text_pre_one.astype(jnp.bfloat16)
    layout_attn_in = layout_pre_one.astype(jnp.bfloat16)
    context_grad = product("sd,tcd->tsc", text_attn_in, out_weight).astype(jnp.bfloat16)
    lcontext_grad = product("sd,tcd->tsc", layout_attn_in, lout_weight).astype(jnp.bfloat16)
    out_grad = product("tsc,sd->tcd", context, text_attn_in)[:, :192].astype(jnp.bfloat16)
    lout_grad = product("tsc,sd->tcd", lcontext, layout_attn_in)
    qkv_in, lqkv_in = attend_back(
        length, qkv, lqkv, log_total, context, lcontext, context_grad, lcontext_grad
    )
    qkv_grad = product("sd,tse->tde", text_low, qkv_in)
    lqkv_grad = product("sd,tse->tde", layout_low, lqkv_in)
    heads_grad, small_grad = pack(qkv_grad, lqkv_grad, lout_grad, lup_grad, ldown_grad)
    if near:
        late = jnp.concatenate(
            (heads_grad, out_grad, up_grad[:, :160], down_grad[:, 592:], small_grad), 1
        )
        late = late.reshape(parts, 78, 16, UNIT)
        late_kept, late_received = core_stage(late, place[3])
        late_sum = plane_stages(late_kept, late_received, ((0, 38), (19, 58)), place)
        kept, received = line_stages(early_sum, late_sum, place)
        span_grad, squares = finish(
            shift, kept.reshape(FRAME, UNIT), received.reshape(FRAME, UNIT)
        )
        local_square = jnp.sum(squares)
    else:
        flat_grad = jnp.concatenate((heads_grad, out_grad, up_grad, down_grad, small_grad), 1)
        flat_grad = flat_grad.reshape(parts * dp_count, -1, 192)
        span_grad = lax.psum_scatter(flat_grad, ("tensor", "dp"), scatter_dimension=0, tiled=True)
        span_grad = span_grad.astype(jnp.float32).reshape(master.shape)
        local_square = jnp.sum(span_grad * span_grad)
    text_full = text_pre_one + over_parts("se,de->sd", qkv_in, qkv_weight)
    layout_full = layout_pre_one + over_parts("se,de->sd", lqkv_in, lqkv_weight)
    text_in_grad = jnp.where(text_flag, 0.0, text_full)
    layout_in_grad = jnp.where(box_flag, 0.0, layout_full)
    text_embed_grad = summed(jnp.where(text_flag, text_full, 0.0))
    layout_embed_grad = summed(jnp.where(box_flag, layout_full, 0.0))
    qkv_sums = jnp.sum(qkv_in, 1, dtype=jnp.float32)
    lqkv_sums = jnp.sum(lqkv_in, 1, dtype=jnp.float32)
    vector_part = jnp.concatenate(
        [
            qkv_sums[:, 0:192].reshape(-1),
            qkv_sums[:, 512:704].reshape(-1),
            summed(text_pre_one),
            text_gain_one,
            text_shift_one,
            summed(text_pre_two),
            text_gain_two,
            text_shift_two,
            jnp.sum(text_up_grad, 1, dtype=jnp.float32).reshape(-1),
            unspaced(lqkv_sums[:, 0:256]),
            unspaced(lqkv_sums[:, 512:768]),
            summed(layout_pre_one),
            layout_gain_one,
            layout_shift_one,
            summed(layout_pre_two),
            layout_gain_two,
            layout_shift_two,
            jnp.sum(layout_up_grad, 1, dtype=jnp.float32).reshape(-1),
            text_embed_grad,
            layout_embed_grad,
        ]
    )
    if near:
        vector_grad = total_of(vector_part)
        matrix_square = total_of(local_square.reshape(1, 1))[0, 0]
    else:
        vector_grad = lax.psum(vector_part, ("dp", "tensor"))
        matrix_square = lax.psum(local_square, ("dp", "tensor"))
    grad_norm = jnp.sqrt(matrix_square + jnp.sum(vector_grad * vector_grad))
    factor = clip_bound / jnp.maximum(grad_norm, clip_bound)
    if near:
        matrix_new = adam(
            (dp_index * span).reshape(1),
            factor.reshape(1),
            master,
            span_grad,
            first_moment,
            second_moment,
            ema_weights,
        )
        matrix_new = tuple(matrix_new)
    else:
        rates = lax.dynamic_slice_in_dim(rate_table(parts), dp_index * span, span)
        matrix_new = adam_update(
            master,
            span_grad,
            first_moment,
            second_moment,
            ema_weights,
            rates.reshape(master.shape),
            factor,
        )
    vector_new = adam_update(
        vectors, vector_grad, vector_first, vector_second, vector_ema, vector_rate, factor
    )
    return (
        (
            text_final.astype(jnp.bfloat16)[None],
            layout_final.astype(jnp.bfloat16)[None],
            text_in_grad[None],
            layout_in_grad[None],
            grad_norm,
        )
        + matrix_new
        + vector_new
    )


def solution(mesh):
    in_specs = (
        P(("dp", "tensor"), None, None),
        P(("dp", "tensor"), None, None),
        P("dp"),
        P(("dp", "tensor"), None),
        P(("dp", "tensor"), None),
        P(("dp", "tensor"), None, None),
        P(("dp", "tensor"), None, None),
        P("tensor", "dp", None),
        P("tensor", "dp", None),
        P("tensor", "dp", None),
        P("tensor", "dp", None),
        P(),
        P(),
        P(),
        P(),
    )
    out_specs = (
        P(("dp", "tensor"), None, None),
        P(("dp", "tensor"), None, None),
        P(("dp", "tensor"), None, None),
        P(("dp", "tensor"), None, None),
        P(),
        P("tensor", "dp", None),
        P("tensor", "dp", None),
        P("tensor", "dp", None),
        P("tensor", "dp", None),
        P("tensor", "dp", None),
        P(),
        P(),
        P(),
        P(),
        P(),
    )
    return jax.shard_map(shards, mesh=mesh, in_specs=in_specs, out_specs=out_specs, check_vma=False)
```

time: 1250 us -> 490 us (0.39)
  waiting for transfers between devices: 610 us -> 204 us
  local copies, waits for them, and re-layouts: 180 us -> 45.3 us
  other arithmetic: 171 us -> 48 us
  matrix products: 183 us -> 80.8 us
  blocking collectives: 76.6 us -> 0 us
  Pallas kernels: 0 us -> 47.8 us
  starting transfers between devices: 1.28 us -> 27.2 us
    reduce_scatter x4 -> x0, waiting for transfers between devices: 267 us -> none  [head_total(): lax.psum_scatter(term_fn(jnp.int32(0), own_pages * lax.axis_size('tensor'...]
    unnamed x11 -> x1, waiting for transfers between devices: 220 us -> 0.02 us
    dot_general x92 -> x48, matrix products: 183 us -> 80.8 us  [product(): return jnp.einsum(spec, left, right, preferred_element_type=jnp.float32)]
    ppermute x0 -> x18, waiting for transfers between devices: none -> 93.8 us  [swap(): return lax.ppermute(value, ('dp', 'tensor'), ROUNDS[step])]
    all_gather x1 -> x0, other arithmetic: 69.3 us -> none  [shards(): gathered = lax.all_gather(wire, 'dp', axis=1, tiled=True)]
    pallas_call x0 -> x7, Pallas kernels: none -> 47.8 us  [the longest x1 15.4 us: attend_back(): pl.pallas_call(attend_back_kernel, grid=(parts,), in_specs=[pl.BlockSpec(...]
    dynamic_slice x63 -> x2, local copies, waits for them, and re-layouts: 47.9 us -> 1.31 us  [the longest x1 0.67 us: block(): return picked(blocks, order[layer], 0)]
    psum x1 -> x0, blocking collectives: 40.2 us -> none  [shards(): matrix_square = lax.psum(local_square, ('dp', 'tensor'))]
  transfers between devices with their start and end apart: 10 -> 19, of which waited for: 8 -> 15; matrix products, arithmetic and copies ran while one was open for 16% -> 8% of each run, Pallas kernels for 0% -> 0%
where the time goes in v1:
time: 490 us; the launch traced here: 482 us
  waiting for transfers between devices  204 us (42%)
  matrix products  80.8 us (16%)
  other arithmetic  48 us (10%)
  Pallas kernels  47.8 us (10%)
  local copies, waits for them, and re-layouts  45.3 us (9%)
  between operations  29.6 us (6%)
  starting transfers between devices  27.2 us (6%)
    all_gather x1, waiting for transfers between devices, shards(): frames = lax.all_gather(frame, ('tensor', 'dp'), axis=0, tiled=True)  110 us
    ppermute x18, waiting for transfers between devices, swap(): return lax.ppermute(value, ('dp', 'tensor'), ROUNDS[step])  93.8 us
    dot_general x48, matrix products, product(): return jnp.einsum(spec, left, right, preferred_element_type=jnp.float32)  80.8 us
    ppermute x18, starting transfers between devices, swap(): return lax.ppermute(value, ('dp', 'tensor'), ROUNDS[step])  27.1 us
    unnamed x152, local copies, waits for them, and re-layouts  17.2 us
    pallas_call x1, Pallas kernels, attend_back(): pl.pallas_call(attend_back_kernel, grid=(parts,), in_specs=[pl.BlockSpec(...  15.4 us
    convert_element_type x9, other arithmetic, added(): (left.astype(jnp.float32) + right.astype(jnp.float32)).astype(jnp.bfloat16)  12.6 us
  transfers between devices with their start and end apart: 19, of which 15 were waited for; matrix products, arithmetic and copies ran while one was open for 8% of the time, Pallas kernels for 0%

profile of v1, /device:TPU:0, one launch (start us, length us, event | category | flops | bytes accessed | tf_op | source)
XLA Modules:
  0.0 482.3 jit_solution(13289316298530610491)
XLA Ops:
  7.3 2.5 cast_frame.1
  14.8 109.7 %all-gather.2.cloned.1.call-done = bf16[32,320,768]{2,1,0:T(8,128)(2,1)} async-done(((bf16[1,320,768]{2,1,0:T(8,128)(2,1)}), bf16[32,320,768]{2,1,0:T(8,128)(2,1)}) %all-gather.2.cloned.1.call-update) | async-done | bytes 15728656 | tf_op jit(solution)/shard_map/all_gather | solution.py:699
  125.4 6.9 %slice.495 = bf16[4,8,288,768]{3,2,1,0:T(8,128)(2,1)S(1)} slice(bf16[4,8,320,768]{3,2,1,0:T(8,128)(2,1)} %bitcast.646), slice={[0:4], [0:8], [16:304], [0:768]} | slice | bytes 28311552 | tf_op jit(solution)/shard_map/slice | solution.py:702
  135.8 5.3 %copy-done.8 = bf16[4,8,304,768]{3,2,1,0:T(8,128)(2,1)} copy-done((bf16[4,8,304,768]{3,2,1,0:T(8,128)(2,1)}, bf16[4,8,304,768]{3,2,1,0:T(8,128)(2,1)S(1)}, u32[]{:S(2)}) %copy-start.8) | copy-done | bytes 14942232
  141.1 8.7 %pad_maximum_fusion.heads_ref.out_ref.small_ref = bf16[4,2448,768]{2,1,0:T(8,128)(2,1)} fusion(bf16[4,16,768]{2,1,0:T(8,128)(2,1)S(1)} %slice_bitcast_fusion.48, bf16[4,2432,768]{2,1,0:T(8,128)(2,1)S(1)} %bitcast.629), kind=kLoop, calls=%fused_computation | loop fusion | flops 30081024 | bytes 30081024 | tf_op jit(solution)/shard_map/concatenate | solution.py:703
  149.8 5.5 %unpack.1 = (bf16[4,768,768]{2,1,0:T(8,128)(2,1)S(1)}, bf16[4,256,768]{2,1,0:T(8,128)(2,1)S(1)}, bf16[4,192,768]{2,1,0:T(8,128)(2,1)S(1)}, bf16[4,256,192]{2,1,0...) custom-call(bf16[4,2448,768]{2,1,0:T(8,128)(2,1)} %pad_maximum_fusion.heads_ref.out_ref.small_ref, ...), custom_call_target="tpu_custom_call" | custom-call | tf_op jit(solution)/shard_map/unpack/pallas_call | solution.py:497
  155.3 3.0 fusion.26.text_ref
  159.6 8.4 %attend.1 = (bf16[4,512,256]{2,1,0:T(8,128)(2,1)S(1)}, bf16[4,512,256]{2,1,0:T(8,128)(2,1)S(1)}, f32[4,8,512]{2,1,0:T(8,128)S(1)}) custom-call(s32[1]{0:T(128)} %dynamic_slice.154.length_ref, bf16[4,512,768]{2,1,0:T(8,128)(2,1)S(1)} %fusion.26.text_ref, bf16[4,512,768]{2,1,0:T(8,128)(2,1)S(1)} %fusion.27.layout_ref), custom_call_target="tpu_custom_call" | custom-call | flops 3221225472 | bytes 10485760 | tf_op jit(solution)/shard_map/attend/pallas_call | solution.py:194
  171.7 19.1 %fusion.9 = (bf16[4,512,768]{2,1,0:T(8,128)(2,1)S(1)}, f32[4,512,768]{2,1,0:T(8,128)}, f32[4,768,512]{1,2,0:T(8,128)}) fusion(f32[4,768]{1,0:T(4,128)S(1)} %add.619, bf16[4,2432,768]{2,1,0:T(8,128)(2,1)S(1)} %bitcast.633, f32[512,768]{1,0:T(8,128)S(1)} %get-tuple-element.153, f32[768]{0:T(1024)S(1)} %get-tuple-element.128, f32[768]{0:T(1024)S(1)} %get-tuple-element.129, ...), kind=kOutput, calls=%fused_computation.20 | convolution fusion | flops 2521694208 | bytes 22044672 | tf_op jit(solution)/shard_map/sd,tde->tse/dot_general | solution.py:714
  195.5 2.7 fusion.241
  198.1 10.2 %convert_reduce_fusion.1 = (f32[4,768]{1,0:T(4,128)}, bf16[4,512,768]{2,1,0:T(8,128)(2,1)}) fusion(f32[4,512,768]{2,1,0:T(8,128)} %get-tuple-element.85, f32[512,768]{1,0:T(8,128)} %get-tuple-element.79, bf16[4,2432,768]{2,1,0:T(8,128)(2,1)S(1)} %bitcast.638, f32[4,768,512]{1,2,0:T(8,128)} %get-tuple-element.154, f32[4,768]{1,0:T(4,128)S(1)} %add.619), kind=kOutput, calls=%fused_computation.22 | convolution fusion | flops 2443047936 | bytes 22044672 | tf_op jit(solution)/shard_map/sd,ted->tse/dot_general | solution.py:714
  208.3 2.1 fusion.75
  213.3 3.7 fusion.52
  226.4 2.9 multiply_reduce_fusion
  232.7 4.7 convert_bitcast_fusion
  237.4 2.9 convolution_convert_fusion
  240.4 15.4 %attend_back.1 = (bf16[4,512,768]{2,1,0:T(8,128)(2,1)S(1)}, bf16[4,512,768]{2,1,0:T(8,128)(2,1)S(1)}) custom-call(s32[1]{0:T(128)} %dynamic_slice.154.length_ref, bf16[4,512,768]{2,1,0:T(8,128)(2,1)S(1)} %fusion.26.text_ref, bf16[4,512,768]{2,1,0:T(8,128)(2,1)} %copy-done.7, f32[4,8,512]{2,1,0:T(8,128)S(1)} %get-tuple-element.43.total_ref, ...), custom_call_target="tpu_custom_call" | custom-call | flops 12884901888 | bytes 20971520 | tf_op jit(solution)/shard_map/attend_back/pallas_call | solution.py:274
  255.9 5.3 %convolution_bitcast_fusion.qkv_ref = f32[4,768,768]{2,1,0:T(8,128)} fusion(bf16[4,512,768]{2,1,0:T(8,128)(2,1)S(1)} %get-tuple-element.44, bf16[1,512,768]{2,1,0:T(8,128)(2,1)S(1)} %copy-done.19, f32[768]{0:T(1024)S(1)} %copy-done.37, pred[512]{0:T(512)(128)(4,1)S(1)} %copy-done.50), kind=kOutput, calls=%fused_computation.48 | convolution fusion | flops 2416705536 | bytes 13372928 | tf_op jit(solution)/shard_map/sd,tse->tde/dot_general | solution.py:714
  262.1 7.1 %pack.1 = (bf16[4,576,768]{2,1,0:T(8,128)(2,1)S(1)}, bf16[4,144,768]{2,1,0:T(8,128)(2,1)S(1)}) custom-call(f32[4,768,768]{2,1,0:T(8,128)} %convolution_bitcast_fusion.qkv_ref, f32[4,192,768]{2,1,0:T(8,128)S(1)} %convolution_bitcast_fusion.1.lqkv_ref, f32[4,256,192]{2,1,0:T(8,128)S(1)} %fusion.193.lwo_ref, ...), custom_call_target="tpu_custom_call" | custom-call | tf_op jit(solution)/shard_map/pack/pallas_call | solution.py:559
  271.2 2.1 slice.526
  275.6 2.2 slice.527
  277.7 6.8 %pad_maximum_fusion.2 = bf16[4,1232,768]{2,1,0:T(8,128)(2,1)} fusion(bf16[4,608,768]{2,1,0:T(8,128)(2,1)} %slice.527, bf16[4,624,768]{2,1,0:T(8,128)(2,1)} %slice.526), kind=kLoop, calls=%fused_computation.3 | loop fusion | flops 15138816 | bytes 15138816 | tf_op jit(solution)/shard_map/concatenate | solution.py:790
  284.5 4.2 dynamic-slice_bitcast_fusion.1
  289.0 2.3 slice_dynamic-update-slice_fusion
  292.3 4.3 dynamic-slice_bitcast_fusion
  307.0 2.3 convert_reduce_fusion.2
  309.7 3.1 fusion.99
  313.2 2.1 collective-permute-start.4
  315.3 3.0 fusion.107
  320.7 2.2 fusion.98
  323.1 2.3 fusion.106
  325.6 12.3 %collective-permute-done.4 = bf16[2,2,20,16,768]{4,3,2,1,0:T(8,128)(2,1)S(1)} collective-permute-done((bf16[2,2,20,16,768]{4,3,2,1,0:T(8,128)(2,1)S(1)}, bf16[2,2,20,16,768]{4,3,2,1,0:T(8,128)(2,1)S(1)}, u32[]{:S(2)}, u32[]{:S(2)}) %collective-permute-start.4) | collective-permute-done | bytes 1966112 | tf_op jit(solution)/shard_map/ppermute | solution.py:597
  340.1 29.4 %collective-permute-done.1 = bf16[2,2,20,16,768]{4,3,2,1,0:T(8,128)(2,1)S(1)} collective-permute-done((bf16[2,2,20,16,768]{4,3,2,1,0:T(8,128)(2,1)S(1)}, bf16[2,2,20,16,768]{4,3,2,1,0:T(8,128)(2,1)S(1)}, u32[]{:S(2)}, u32[]{:S(2)}) %collective-permute-start.1) | collective-permute-done | bytes 1966112 | tf_op jit(solution)/shard_map/ppermute | solution.py:597
  374.2 10.2 %collective-permute-done.2 = bf16[2,20,16,768]{3,2,1,0:T(8,128)(2,1)S(1)} collective-permute-done((bf16[2,20,16,768]{3,2,1,0:T(8,128)(2,1)S(1)}, bf16[2,20,16,768]{3,2,1,0:T(8,128)(2,1)S(1)}, u32[]{:S(2)}, u32[]{:S(2)}) %collective-permute-start.2) | collective-permute-done | bytes 983072 | tf_op jit(solution)/shard_map/ppermute | solution.py:597
  390.6 2.2 select_reduce_fusion
  392.7 25.2 %collective-permute-done.6 = bf16[2,20,16,768]{3,2,1,0:T(8,128)(2,1)S(1)} collective-permute-done((bf16[2,20,16,768]{3,2,1,0:T(8,128)(2,1)S(1)}, bf16[2,20,16,768]{3,2,1,0:T(8,128)(2,1)S(1)}, u32[]{:S(2)}, u32[]{:S(2)}) %collective-permute-start.6) | collective-permute-done | bytes 983072 | tf_op jit(solution)/shard_map/ppermute | solution.py:597
  421.1 2.7 collective-permute-start.14
  423.9 2.1 collective-permute-done.14
  427.5 2.7 collective-permute-done.15
  431.2 4.1 collective-permute-done.16
  435.3 2.3 collective-permute-start.17
  437.6 2.1 collective-permute-done.17
  441.1 2.6 finish.1
  447.5 3.6 collective-permute-start.9
  451.9 2.8 collective-permute-start.10
  456.1 2.4 collective-permute-start.11
  461.2 3.4 collective-permute-start.12
  467.5 6.4 %adam.1 = (f32[1,1,235008]{2,1,0:T(1,128)}, f32[1,1,235008]{2,1,0:T(1,128)}, f32[1,1,235008]{2,1,0:T(1,128)}, bf16[1,1,235008]{2,1,0:T(2,128)(2,1)}, f32[1,1,235008]{2,1,0:T(1,128)}) custom-call(s32[1]{0:T(128)} %bitcast.140.first_index_ref, f32[1]{0:T(128)} %bitcast.141.factor_ref, f32[1,1,235008]{2,1,0:T(1,128)} %weight_ref.1, ...), custom_call_target="tpu_custom_call" | custom-call | tf_op jit(solution)/shard_map/adam/pallas_call | solution.py:424
  (308 shorter events, 73.4 us)
Async XLA Ops:
  7.2 5.4 %copy-start.14 = (bf16[1,512,192]{1,2,0:T(8,128)(2,1)S(1)}, bf16[1,512,192]{1,2,0:T(8,128)(2,1)}, u32[]{:S(2)}) copy-start(bf16[1,512,192]{1,2,0:T(8,128)(2,1)} %param.23) | copy-start | bytes 589828
  7.2 6.1 %copy-start.9 = (bf16[1,512,768]{2,1,0:T(8,128)(2,1)S(1)}, bf16[1,512,768]{2,1,0:T(8,128)(2,1)}, u32[]{:S(2)}) copy-start(bf16[1,512,768]{2,1,0:T(8,128)(2,1)} %param.22) | copy-start | bytes 2359300
  7.3 117.2 %all-gather.2.cloned.1.call-start = ((), (), s32[]{:S(2)}) async-start(), calls=%async_computation | async-start | bytes 16220160 | tf_op jit(solution)/shard_map/all_gather | solution.py:699
  9.8 159.2 %copy-start.36 = (f32[768]{0:T(1024)}, f32[768]{0:T(1024)S(1)}, u32[]{:S(2)}) copy-start(f32[768]{0:T(1024)S(1)} %get-tuple-element.133) | copy-start | bytes 9220
  9.8 183.3 %copy-start.38 = (f32[768]{0:T(1024)}, f32[768]{0:T(1024)S(1)}, u32[]{:S(2)}) copy-start(f32[768]{0:T(1024)S(1)} %get-tuple-element.128) | copy-start | bytes 9220
  10.7 121.6 %copy-start.30 = (f32[192]{0:T(256)}, f32[192]{0:T(256)S(1)}, u32[]{:S(2)}) copy-start(f32[192]{0:T(256)S(1)} %get-tuple-element.115) | copy-start | bytes 2308
  10.7 202.2 %copy-start.43 = (f32[192]{0:T(256)}, f32[192]{0:T(256)S(1)}, u32[]{:S(2)}) copy-start(f32[192]{0:T(256)S(1)} %get-tuple-element.122) | copy-start | bytes 2308
  12.6 156.5 %copy-start.49 = (pred[512]{0:T(512)(128)(4,1)}, pred[512]{0:T(512)(128)(4,1)S(1)}, u32[]{:S(2)}) copy-start(pred[512]{0:T(512)(128)(4,1)S(1)} %compare_reduce_fusion.1) | copy-start | bytes 1540
  12.6 200.3 %copy-start.46 = (pred[512]{0:T(512)(128)(4,1)}, pred[512]{0:T(512)(128)(4,1)S(1)}, u32[]{:S(2)}) copy-start(pred[512]{0:T(512)(128)(4,1)S(1)} %compare_reduce_fusion) | copy-start | bytes 1540
  149.8 5.5 %copy-start.18 = (bf16[1,512,768]{2,1,0:T(8,128)(2,1)S(1)}, bf16[1,512,768]{2,1,0:T(8,128)(2,1)}, u32[]{:S(2)}) copy-start(bf16[1,512,768]{2,1,0:T(8,128)(2,1)} %param.17) | copy-start | bytes 2359300
  159.5 8.4 %copy-start.7 = (bf16[4,512,768]{2,1,0:T(8,128)(2,1)}, bf16[4,512,768]{2,1,0:T(8,128)(2,1)S(1)}, u32[]{:S(2)}) copy-start(bf16[4,512,768]{2,1,0:T(8,128)(2,1)S(1)} %fusion.27.layout_ref) | copy-start | bytes 9437188
  159.5 10.7 %slice-start.2 = ((s8[14942208]{0:T(1024)(128)(4,1)}), s8[4194304]{0:T(1024)(128)(4,1)S(1)}, s32[]{:S(2)}) async-start(s8[14942208]{0:T(1024)(128)(4,1)} %bitcast.631), calls=%async_computation.3 | async-start | bytes 8388608
  159.6 10.7 %slice-start.3 = ((s8[14942208]{0:T(1024)(128)(4,1)}), s8[2359296]{0:T(1024)(128)(4,1)S(1)}, s32[]{:S(2)}) async-start(s8[14942208]{0:T(1024)(128)(4,1)} %bitcast.631), calls=%async_computation.4 | async-start | bytes 4718592
  240.4 35.2 %copy-start.13 = (bf16[4,768,768]{2,1,0:T(8,128)(2,1)}, bf16[4,768,768]{2,1,0:T(8,128)(2,1)S(1)}, u32[]{:S(2)}) copy-start(bf16[4,768,768]{2,1,0:T(8,128)(2,1)S(1)} %convolution_convert_fusion) | copy-start | bytes 14155780
  240.4 15.4 %copy-start.19 = (bf16[1,512,768]{2,1,0:T(8,128)(2,1)S(1)}, bf16[1,512,768]{2,1,0:T(8,128)(2,1)}, u32[]{:S(2)}) copy-start(bf16[1,512,768]{2,1,0:T(8,128)(2,1)} %param.17) | copy-start | bytes 2359300
  240.4 15.4 %copy-start.37 = (f32[768]{0:T(1024)S(1)}, f32[768]{0:T(1024)}, u32[]{:S(2)}) copy-start(f32[768]{0:T(1024)} %copy-done.36) | copy-start | bytes 9220
  240.4 15.4 %copy-start.50 = (pred[512]{0:T(512)(128)(4,1)S(1)}, pred[512]{0:T(512)(128)(4,1)}, u32[]{:S(2)}) copy-start(pred[512]{0:T(512)(128)(4,1)} %copy-done.49) | copy-start | bytes 1540
  255.8 5.4 %copy-start = (bf16[4,512,768]{2,1,0:T(8,128)(2,1)}, bf16[4,512,768]{2,1,0:T(8,128)(2,1)S(1)}, u32[]{:S(2)}) copy-start(bf16[4,512,768]{2,1,0:T(8,128)(2,1)S(1)} %get-tuple-element.44) | copy-start | bytes 9437188
  255.8 5.4 %copy-start.17 = (bf16[1,512,192]{1,2,0:T(8,128)(2,1)S(1)}, bf16[1,512,192]{1,2,0:T(8,128)(2,1)}, u32[]{:S(2)}) copy-start(bf16[1,512,192]{1,2,0:T(8,128)(2,1)} %param.18) | copy-start | bytes 589828
  255.8 5.3 %copy-start.44 = (f32[192]{0:T(256)S(1)}, f32[192]{0:T(256)}, u32[]{:S(2)}) copy-start(f32[192]{0:T(256)} %copy-done.43) | copy-start | bytes 2308
  255.9 5.3 %copy-start.47 = (pred[512]{0:T(512)(128)(4,1)S(1)}, pred[512]{0:T(512)(128)(4,1)}, u32[]{:S(2)}) copy-start(pred[512]{0:T(512)(128)(4,1)} %copy-done.46) | copy-start | bytes 1540
  261.2 10.0 %slice-start.6 = ((s8[4718592]{0:T(1024)(128)(4,1)}), s8[4194304]{0:T(1024)(128)(4,1)S(1)}, s32[]{:S(2)}) async-start(s8[4718592]{0:T(1024)(128)(4,1)} %bitcast.649), calls=%async_computation.7 | async-start | bytes 8388608
  262.1 9.2 %slice-start.7 = ((s8[4718592]{0:T(1024)(128)(4,1)}), s8[524288]{0:T(1024)(128)(4,1)S(1)}, s32[]{:S(2)}) async-start(s8[4718592]{0:T(1024)(128)(4,1)} %bitcast.649), calls=%async_computation.8 | async-start | bytes 1048576
  288.7 21.0 %collective-permute-start.3 = (bf16[2,77,16,768]{3,2,1,0:T(8,128)(2,1)}, bf16[2,77,16,768]{3,2,1,0:T(8,128)(2,1)}, u32[]{:S(2)}, u32[]{:S(2)}) collective-permute-start(bf16[2,77,16,768]{3,2,1,0:T(8,128)(2,1)} %dynamic-slice_bitcast_fusion.1), channel_id=1, source_target_pairs={{0,1},{1,0},{2,3},{3,2},{4,5},{5,4},{6,7},{7,6},{8,9},{9,8},{10,11... | collective-permute-start | bytes 11354120 | tf_op jit(solution)/shard_map/ppermute | solution.py:597
  296.6 18.8 %collective-permute-start = (bf16[2,78,16,768]{3,2,1,0:T(8,128)(2,1)}, bf16[2,78,16,768]{3,2,1,0:T(8,128)(2,1)}, u32[]{:S(2)}, u32[]{:S(2)}) collective-permute-start(bf16[2,78,16,768]{3,2,1,0:T(8,128)(2,1)} %dynamic-slice_bitcast_fusion), channel_id=1, source_target_pairs={{0,1},{1,0},{2,3},{3,2},{4,5},{5,4},{6,7},{7,6},{8,9},{9,8},{10,11... | collective-permute-start | bytes 11501576 | tf_op jit(solution)/shard_map/ppermute | solution.py:597
  313.2 24.7 %collective-permute-start.4 = (bf16[2,2,20,16,768]{4,3,2,1,0:T(8,128)(2,1)S(1)}, bf16[2,2,20,16,768]{4,3,2,1,0:T(8,128)(2,1)S(1)}, u32[]{:S(2)}, u32[]{:S(2)}) collective-permute-start(bf16[2,2,20,16,768]{4,3,2,1,0:T(8,128)(2,1)S(1)} %pad_maximum_fusion.4), channel_id=1, source_target_pairs={{0,4},{1,3},{2,6},{3,1},{4,0},{5,7},{6,2},{7,5},{8,12},{9,11},{10,... | collective-permute-start | bytes 5898248 | tf_op jit(solution)/shard_map/ppermute | solution.py:597
  318.8 50.8 %collective-permute-start.1 = (bf16[2,2,20,16,768]{4,3,2,1,0:T(8,128)(2,1)S(1)}, bf16[2,2,20,16,768]{4,3,2,1,0:T(8,128)(2,1)S(1)}, u32[]{:S(2)}, u32[]{:S(2)}) collective-permute-start(bf16[2,2,20,16,768]{4,3,2,1,0:T(8,128)(2,1)S(1)} %pad_maximum_fusion.3), channel_id=1, source_target_pairs={{0,4},{1,3},{2,6},{3,1},{4,0},{5,7},{6,2},{7,5},{8,12},{9,11},{10,... | collective-permute-start | bytes 5898248 | tf_op jit(solution)/shard_map/ppermute | solution.py:597
  323.1 49.2 %slice-start = ((s8[4718592]{0:T(1024)(128)(4,1)}), s8[4194304]{0:T(1024)(128)(4,1)S(1)}, s32[]{:S(2)}) async-start(s8[4718592]{0:T(1024)(128)(4,1)} %bitcast.627), calls=%async_computation.1 | async-start | bytes 8388608
  325.6 46.7 %slice-start.1 = ((s8[4718592]{0:T(1024)(128)(4,1)}), s8[524288]{0:T(1024)(128)(4,1)S(1)}, s32[]{:S(2)}) async-start(s8[4718592]{0:T(1024)(128)(4,1)} %bitcast.627), calls=%async_computation.2 | async-start | bytes 1048576
  338.6 35.3 %collective-permute-start.5 = (bf16[2,20,16,768]{3,2,1,0:T(8,128)(2,1)S(1)}, bf16[2,20,16,768]{3,2,1,0:T(8,128)(2,1)S(1)}, u32[]{:S(2)}, u32[]{:S(2)}) collective-permute-start(bf16[2,20,16,768]{3,2,1,0:T(8,128)(2,1)S(1)} %dynamic-slice_bitcast_fusion.2), channel_id=1, source_target_pairs={{0,2},{1,5},{2,0},{3,7},{4,6},{5,1},{6,4},{7,3},{8,10},{9,13},{10,... | collective-permute-start | bytes 2949128 | tf_op jit(solution)/shard_map/ppermute | solution.py:597
  370.2 14.2 %collective-permute-start.2 = (bf16[2,20,16,768]{3,2,1,0:T(8,128)(2,1)S(1)}, bf16[2,20,16,768]{3,2,1,0:T(8,128)(2,1)S(1)}, u32[]{:S(2)}, u32[]{:S(2)}) collective-permute-start(bf16[2,20,16,768]{3,2,1,0:T(8,128)(2,1)S(1)} %dynamic-slice_bitcast_fusion.3), channel_id=1, source_target_pairs={{0,2},{1,5},{2,0},{3,7},{4,6},{5,1},{6,4},{7,3},{8,10},{9,13},{10,... | collective-permute-start | bytes 2949128 | tf_op jit(solution)/shard_map/ppermute | solution.py:597
  385.5 32.4 %collective-permute-start.6 = (bf16[2,20,16,768]{3,2,1,0:T(8,128)(2,1)S(1)}, bf16[2,20,16,768]{3,2,1,0:T(8,128)(2,1)S(1)}, u32[]{:S(2)}, u32[]{:S(2)}) collective-permute-start(bf16[2,20,16,768]{3,2,1,0:T(8,128)(2,1)S(1)} %pad_maximum_fusion.5), channel_id=1, source_target_pairs={{0,16},{1,9},{2,18},{3,11},{4,20},{5,13},{6,22},{7,15},{8,24},{9,1... | collective-permute-start | bytes 2949128 | tf_op jit(solution)/shard_map/ppermute | solution.py:597
  418.3 47.8 %copy-start.22 = (f32[12480]{0:T(1024)S(1)}, f32[12480]{0:T(1024)}, u32[]{:S(2)}) copy-start(f32[12480]{0:T(1024)} %param.28) | copy-start | bytes 149764
  418.3 47.8 %copy-start.27 = (f32[12480]{0:T(1024)S(1)}, f32[12480]{0:T(1024)}, u32[]{:S(2)}) copy-start(f32[12480]{0:T(1024)} %param.31) | copy-start | bytes 149764
  418.3 47.8 %copy-start.28 = (f32[12480]{0:T(1024)S(1)}, f32[12480]{0:T(1024)}, u32[]{:S(2)}) copy-start(f32[12480]{0:T(1024)} %param.29) | copy-start | bytes 149764
  418.4 47.8 %copy-start.29 = (f32[12480]{0:T(1024)S(1)}, f32[12480]{0:T(1024)}, u32[]{:S(2)}) copy-start(f32[12480]{0:T(1024)} %param.30) | copy-start | bytes 149764
  419.2 21.1 %collective-permute-start.7 = (bf16[20,16,768]{2,1,0:T(8,128)(2,1)S(1)}, bf16[20,16,768]{2,1,0:T(8,128)(2,1)S(1)}, u32[]{:S(2)}, u32[]{:S(2)}) collective-permute-start(bf16[20,16,768]{2,1,0:T(8,128)(2,1)S(1)} %get-tuple-element.109), channel_id=1, source_target_pairs={{0,8},{1,17},{2,10},{3,19},{4,12},{5,21},{6,14},{7,23},{8,0},{9,25... | collective-permute-start | bytes 1474568 | tf_op jit(solution)/shard_map/ppermute | solution.py:597
  419.9 1.3 collective-permute-start.13
  421.1 4.9 %collective-permute-start.14 = (f32[12480]{0:T(1024)S(1)}, f32[12480]{0:T(1024)S(1)}, u32[]{:S(2)}, u32[]{:S(2)}) collective-permute-start(f32[12480]{0:T(1024)S(1)} %add.719), channel_id=1, source_target_pairs={{0,4},{1,3},{2,6},{3,1},{4,0},{5,7},{6,2},{7,5},{8,12},{9,11},{10,... | collective-permute-start | bytes 149768 | tf_op jit(solution)/shard_map/ppermute | solution.py:597
  426.0 4.2 collective-permute-start.15
  430.2 5.1 %collective-permute-start.16 = (f32[12480]{0:T(1024)S(1)}, f32[12480]{0:T(1024)S(1)}, u32[]{:S(2)}, u32[]{:S(2)}) collective-permute-start(f32[12480]{0:T(1024)S(1)} %add.721), channel_id=1, source_target_pairs={{0,16},{1,9},{2,18},{3,11},{4,20},{5,13},{6,22},{7,15},{8,24},{9,1... | collective-permute-start | bytes 149768 | tf_op jit(solution)/shard_map/ppermute | solution.py:597
  435.3 4.4 collective-permute-start.17
  445.0 1.2 collective-permute-start.8
  447.5 3.8 collective-permute-start.9
  451.9 3.6 collective-permute-start.10
  456.1 4.5 collective-permute-start.11
  461.2 3.6 collective-permute-start.12
  466.8 7.1 %copy-start.23 = (f32[12480]{0:T(1024)}, f32[12480]{0:T(1024)S(1)}, u32[]{:S(2)}) copy-start(f32[12480]{0:T(1024)S(1)} %get-tuple-element.72) | copy-start | bytes 149764
  (46 other events, 93.4 us)
Sparse Core Ops, SparseCore 0:
  11.7 112.7 all-gather.1
